TPU v7x, 128 devices: a whole 4x4x4 slice. The times are simulated.
128 devices in a mesh: line: 8 (over y, core), bus: 16 (over x, z).
Axes of the slice: x: 4, y: 4, z: 4, core: 2. Of those that a mesh axis runs over, the one named last changes fastest.
Arguments:
- site_values: float32 [512, 65536], P('line', 'bus'), may hold values from -6 to 6
- site_bus: int32 [65536], replicated, may hold values from 0 to 71679, as said below
- block_count: int32 [88, 16], P('line', 'bus'), may hold values from 0 to 3
- block_zone: int32 [88, 48], P('line', 'bus'), may hold values from 0 to 6, as said below
- ptdf_blocks: bfloat16 [88, 48, 512, 640], P('line', 'bus'), may hold values from -0.0625 to 0.0625
- rating: float32 [45056], P('line'), may hold values from 0.5 to 4
Outputs:
- loading: float32 [512, 45056], P('bus', 'line')
- worst: float32 [45056], P('line')
Inputs may be any that keep to these rules, and one draw needn't show every extreme that they name: `site_bus`: every aligned block of 4096 sites holds exactly 256 sites whose bus lies in each bus group, the range of 4480 consecutive buses; bus 0 and the last bus each carry a site. `block_zone`: for each line zone, the 3 slots of one bus group name distinct zones of that group.
All inputs are finite; a program needn't handle non-finite values.
Results may differ from a plain program's by a relative error of at most 0.015.
Values may be sent and summed in bfloat16 or wider, within the bound.
A program may use at most 128 MiB of HBM per device.

v0:
```python
import jax
import jax.numpy as jnp
from jax import lax
from jax.sharding import PartitionSpec as P

NB = 71680


def body(site_values, site_bus, block_count, block_zone, ptdf_blocks, rating):
    here = lax.axis_index("bus")
    groups = lax.axis_size("bus")
    scen_part, site_dev = site_values.shape
    bus_dev = NB // groups
    own_ids = lax.dynamic_slice_in_dim(site_bus, here * site_dev, site_dev)
    order = jnp.argsort(own_ids // bus_dev, stable=True)
    outgoing = jnp.take(site_values, order, axis=1)
    sorted_offsets = (jnp.take(own_ids, order) % bus_dev).astype(jnp.float32)
    per_group = site_dev // groups
    grouped_vals = jnp.transpose(outgoing.reshape(scen_part, groups, per_group), (1, 0, 2))
    grouped_offs = sorted_offsets.reshape(groups, per_group)
    columns = jnp.arange(bus_dev).astype(jnp.float32)

    def one_group(carry, inputs):
        vals, offs = inputs
        table = (offs[:, None] == columns[None, :]).astype(jnp.float32)
        return (
            carry,
            jnp.dot(
                vals, table, precision=lax.Precision.HIGHEST, preferred_element_type=jnp.float32
            ),
        )

    _, spread = lax.scan(one_group, jnp.float32(0.0), (grouped_vals, grouped_offs))
    every_bus = jnp.transpose(spread, (1, 0, 2)).reshape(scen_part, groups * bus_dev)
    partial_value = lax.psum_scatter(
        every_bus.astype(jnp.bfloat16), "bus", scatter_dimension=1, tiled=True
    )
    injection = lax.all_gather(partial_value, "line", axis=0, tiled=True)
    zones_dev, slots_dev = block_zone.shape
    line_zone = ptdf_blocks.shape[2]
    zone_width = ptdf_blocks.shape[3]
    bus_zones = bus_dev // zone_width
    count_col = block_count[:, 0]
    scen_total = injection.shape[0]
    rows_here = injection.reshape(
        lax.axis_size("bus") * (scen_total // groups), bus_zones, zone_width
    )

    def one_zone(carry, inputs):
        live_count, zones, blocks = inputs
        total = jnp.zeros((lax.axis_size("bus") * (scen_total // groups), line_zone), jnp.float32)
        for slot in range(slots_dev):
            piece = lax.dynamic_index_in_dim(rows_here, zones[slot], 1, keepdims=False)
            block = blocks[slot]
            product = lax.dot_general(
                piece, block, (((1,), (1,)), ((), ())), preferred_element_type=jnp.float32
            )
            total = total + (slot < live_count).astype(jnp.float32) * product
        return (carry, total)

    _, stacked = lax.scan(one_zone, jnp.float32(0.0), (count_col, block_zone, ptdf_blocks))
    flow = lax.psum_scatter(
        jnp.transpose(stacked, (1, 0, 2))
        .reshape(lax.axis_size("bus") * (scen_total // groups), zones_dev * line_zone)
        .astype(jnp.bfloat16),
        "bus",
        scatter_dimension=0,
        tiled=True,
    ).astype(jnp.float32)
    loading = flow / rating[None, :]
    local_worst = jnp.max(jnp.abs(loading), axis=0)
    worst = lax.pmax(local_worst, "bus")
    return (loading, worst)


def solution(mesh):
    return jax.shard_map(
        body,
        mesh=mesh,
        in_specs=(
            P("line", "bus"),
            P(),
            P("line", "bus"),
            P("line", "bus"),
            P("line", "bus", None, None),
            P("line"),
        ),
        out_specs=(P("bus", "line"), P("line")),
        check_vma=False,
    )
```

profile of v0, /device:TPU:0, one launch (start us, length us, event | category | flops | bytes accessed | tf_op | source)
XLA Modules:
  0.0 633.4 jit_solution(15503625299696602147)
XLA Ops:
  8.0 5.8 sort.17
  13.8 23.0 %gather_fusion.1 = s32[4096]{0:T(1024)S(1)} fusion(s32[4096]{0:T(1024)S(1)} %get-tuple-element.122, s32[4096]{0:T(1024)S(1)} %fusion.23), kind=kCustom, calls=%fused_computation.1 | custom fusion | bytes 49152 | tf_op jit(solution)/shard_map/jit(_take)/gather | solution.py:17
  37.5 14.1 %gather_fusion = f32[4096,64]{1,0:T(8,128)} fusion(f32[64,4096]{0,1:T(8,128)S(1)} %copy.25, s32[4096]{0:T(1024)S(1)} %fusion.23), kind=kCustom, calls=%fused_computation | custom fusion | bytes 2113536 | tf_op jit(solution)/shard_map/jit(_take)/gather | solution.py:16
  51.6 2.2 copy.26
  53.9 39.8 %while.22 = (s32[]{:T(128)}, bf16[16,64,4480]{2,1,0:T(8,128)(2,1)}, f32[16,64,256]{2,1,0:T(8,128)S(1)}, f32[16,256]{1,0:T(8,128)S(1)}, s32[]{:T(128)}) while((s32[]{:T(128)}, bf16[16,64,4480]{2,1,0:T(8,128)(2,1)}, f32[16,64,256]{2,1,0:T(8,128)S(1)}, f32[16,256]{1,0:T(8,128)S(1)}, s32[]{:T(128)}) %tuple.50), condition=%wide.region_2.3_spmd.clone, body=%wide.region_1.2_spmd.clone.sunk | while | flops 881955200 | bytes 1254977 | solution.py:33
  53.9 2.5 fusion.42
  56.4 2.5 fusion.42
  58.9 2.5 fusion.42
  61.3 2.5 fusion.42
  63.8 2.5 fusion.42
  66.3 2.5 fusion.42
  68.8 2.5 fusion.42
  71.2 2.5 fusion.42
  73.7 2.5 fusion.42
  76.2 2.5 fusion.42
  78.7 2.5 fusion.42
  81.1 2.5 fusion.42
  83.7 2.5 fusion.42
  86.2 2.5 fusion.42
  88.7 2.5 fusion.42
  91.2 2.5 fusion.42
  93.6 17.3 %copy.36 = bf16[64,16,4480]{0,2,1:T(8,128)(2,1)} copy(bf16[64,16,4480]{2,0,1:T(8,128)(2,1)} %bitcast.86) | data formatting | bytes 18350080
  111.0 121.2 %reduce-scatter.7.cloned.1.call-done = bf16[4480,64]{1,0:T(8,128)(2,1)} async-done(((bf16[71680,64]{1,0:T(8,128)(2,1)}), bf16[4480,64]{1,0:T(8,128)(2,1)}) %reduce-scatter.7.cloned.1.call-update) | async-done | bytes 573456
  232.2 2.2 copy.33
  234.5 33.3 %all-gather.2.cloned.1.call-done = bf16[512,4480]{1,0:T(8,128)(2,1)} async-done(((bf16[64,4480]{1,0:T(8,128)(2,1)}), bf16[512,4480]{1,0:T(8,128)(2,1)}) %all-gather.2.cloned.1.call-update) | async-done | bytes 4587536 | tf_op jit(solution)/shard_map/all_gather | solution.py:38
  267.8 6.6 %copy.28 = bf16[512,4480]{0,1:T(8,128)(2,1)} copy(bf16[512,4480]{1,0:T(8,128)(2,1)} %all-gather.2.cloned.1.call-done) | data formatting | bytes 9175040 | tf_op jit(solution)/shard_map/all_gather | solution.py:38
  274.4 7.3 %copy.29 = bf16[512,7,640]{2,0,1:T(8,128)(2,1)} copy(bf16[512,7,640]{0,2,1:T(8,128)(2,1)} %bitcast.85) | data formatting | bytes 9175040 | tf_op jit(solution)/shard_map/while | solution.py:61
  281.7 175.0 %while.21 = (s32[]{:T(128)}, bf16[11,512,512]{1,2,0:T(8,128)(2,1)}, s32[11]{0:T(128)S(1)}, s32[11,3]{0,1:T(4,128)S(1)}, bf16[512,7,640]{2,0,1:T(8,128)(2,1)}, /*...) while((s32[]{:T(128)}, bf16[11,512,512]{1,2,0:T(8,128)(2,1)}, ...), condition=%wide.region_5.6_spmd, body=%wide.region_4.5_spmd.sunk | while | flops 1008205824 | bytes 10751873 | solution.py:61
  285.8 1.9 convolution_multiply_fusion.4
  290.1 1.9 fusion.38
  294.6 1.9 fusion.39
  301.7 1.9 convolution_multiply_fusion.4
  306.0 1.9 fusion.38
  310.5 1.9 fusion.39
  317.6 1.9 convolution_multiply_fusion.4
  321.9 1.9 fusion.38
  326.4 1.9 fusion.39
  333.5 1.9 convolution_multiply_fusion.4
  337.8 1.9 fusion.38
  342.3 1.9 fusion.39
  349.4 1.9 convolution_multiply_fusion.4
  353.7 1.9 fusion.38
  358.3 1.9 fusion.39
  365.3 1.9 convolution_multiply_fusion.4
  369.6 1.9 fusion.38
  374.2 1.9 fusion.39
  385.5 1.9 fusion.38
  390.1 1.9 fusion.39
  397.2 1.9 convolution_multiply_fusion.4
  401.4 1.9 fusion.38
  406.0 1.9 fusion.39
  417.4 1.9 fusion.38
  421.9 1.9 fusion.39
  429.0 1.9 convolution_multiply_fusion.4
  433.3 1.9 fusion.38
  437.8 1.9 fusion.39
  444.9 1.9 convolution_multiply_fusion.4
  449.2 1.9 fusion.38
  453.7 1.9 fusion.39
  456.7 8.4 %copy.34 = bf16[512,5632]{1,0:T(8,128)(2,1)} copy(bf16[512,5632]{0,1:T(8,128)(2,1)} %bitcast.87) | data formatting | bytes 11534336
  465.2 81.1 %reduce-scatter.9.cloned.1.call-done = bf16[32,5632]{1,0:T(8,128)(2,1)} async-done(((bf16[512,5632]{1,0:T(8,128)(2,1)}), bf16[32,5632]{1,0:T(8,128)(2,1)}) %reduce-scatter.9.cloned.1.call-update) | async-done | bytes 360464
  546.3 2.4 copy.35
  548.6 4.4 abs_reduce_fusion
  554.8 72.1 %pmax.7 = f32[5632]{0:T(1024)} all-reduce(f32[5632]{0:T(1024)S(1)} %get-tuple-element.119), channel_id=1, replica_groups=mesh['line'=8,'bus'=16] {'bus'}, use_global_device_ids=true, to_apply=%region_8.9 | all-reduce | flops 5632 | bytes 45056 | tf_op jit(solution)/shard_map/pmax | solution.py:72
  (115 shorter events, 33.9 us)
Async XLA Ops:
  7.2 225.0 %reduce-scatter.7.cloned.1.call-start = ((), (), s32[]{:S(2)}) async-start(), calls=%async_computation.3 | async-start | bytes 19496960
  13.8 23.1 %copy-start = (f32[64,4096]{1,0:T(8,128)S(1)}, f32[64,4096]{1,0:T(8,128)}, u32[]{:S(2)}) copy-start(f32[64,4096]{1,0:T(8,128)} %param.10) | copy-start | bytes 3145732
  110.9 156.9 %all-gather.2.cloned.1.call-start = ((), (), s32[]{:S(2)}) async-start(), calls=%async_computation.2 | async-start | bytes 5160960 | tf_op jit(solution)/shard_map/all_gather | solution.py:38
  234.4 311.9 %reduce-scatter.9.cloned.1.call-start = ((), (), s32[]{:S(2)}) async-start(), calls=%async_computation.4 | async-start | bytes 6127616
  274.4 7.3 %copy-start.1 = (s32[11,3]{0,1:T(4,128)S(1)}, s32[11,3]{0,1:T(4,128)}, u32[]{:S(2)}) copy-start(s32[11,3]{0,1:T(4,128)} %param.13) | copy-start | bytes 400
  274.4 7.3 %copy-start.3 = (s32[11,1]{0,1:T(1,128)S(1)}, s32[11,1]{0,1:T(1,128)}, u32[]{:S(2)}) copy-start(s32[11,1]{0,1:T(1,128)} %param.12) | copy-start | bytes 136
  465.1 83.5 %copy-start.2 = (f32[5632]{0:T(1024)S(1)}, f32[5632]{0:T(1024)}, u32[]{:S(2)}) copy-start(f32[5632]{0:T(1024)} %param.15) | copy-start | bytes 67588
Sparse Core Ops, SparseCore 0:
  111.1 121.0 reduce-scatter.6
  234.5 33.2 all-gather.1
  465.3 80.9 reduce-scatter.8
where the time goes:
time: 637 us; the launch traced here: 633 us
  waiting for transfers between devices  236 us (37%)
  local copies, waits for them, and re-layouts  112 us (18%)
  matrix products  102 us (16%)
  loops' own time  86.1 us (14%)
  blocking collectives  72.1 us (11%)
  between operations  13.9 us (2%)
  other arithmetic  11.1 us (2%)
    unnamed x5, waiting for transfers between devices  202 us
    another operation x1, loops' own time, body(): lax.scan(one_zone, jnp.float32(0.0), (count_col, block_zone, ptdf_blocks))  86.1 us
    pmax x1, blocking collectives, body(): worst = lax.pmax(local_worst, 'bus')  72.1 us
    dot_general x33, matrix products, one_zone(): lax.dot_general(piece, block, (((1,), (1,)), ((), ())), preferred_element...  62.5 us
    dot_general x16, matrix products, one_group(): jnp.dot(vals, table, precision=lax.Precision.HIGHEST, preferred_element_t...  39.5 us
    all_gather x1, waiting for transfers between devices, body(): injection = lax.all_gather(partial_value, 'line', axis=0, tiled=True)  33.3 us
    unnamed x14, local copies, waits for them, and re-layouts  32.7 us
    gather x2, local copies, waits for them, and re-layouts, body(): sorted_offsets = (jnp.take(own_ids, order) % bus_dev).astype(jnp.float32)  23 us
  transfers between devices with their start and end apart: 3, of which 3 were waited for; matrix products, arithmetic and copies ran while one was open for 0% of the time, Pallas kernels for 0%

commit v1 on v0

v1 whole, which is shorter than its diff:
```python
import functools

import jax
import jax.numpy as jnp
from jax import lax
from jax.experimental import pallas as pl
from jax.experimental.pallas import tpu as pltpu
from jax.sharding import PartitionSpec as P

MESH = pl.DeviceIdType.MESH
F32 = jnp.float32
BF16 = jnp.bfloat16

LINES = 8
BUSES = 16
RING = 4
BUS_DEV = 4480
SCEN_DEV = 64
SITE_DEV = 4096
PER = 256
ROWS = 80
CHUNKS = SITE_DEV // 128
ZONES = 7
ZB = 640
LZ = 11
ZL = 512
SLOTS = 3
HALF = 256
T = 2 * LZ
NT = (((1,), (1,)), ((), ()))
LAG = (2, 4, 6, 8)
WSPLIT = 8


def iota(shape, dim):
    return lax.broadcasted_iota(jnp.int32, shape, dim).astype(F32)


def kernel(
    count_ref, zone_ref, values_hbm, bus_hbm, blocks_hbm, rating_ref,
    load_ref, worst_ref,
    ids, grp, hi, lo, xa, g01, pre, bt, lhs, sv, rv, blk, inj0, inj1,
    flows, ra, rb, sa, rc, rd, wl, wr,
    in_sem, blk_sem, xs_sem, xr_sem, gs_sem, gr_sem, fs_sem, fr_sem, ws_sem, wr_sem,
):
    line = lax.axis_index("line")
    bus = lax.axis_index("bus")
    y, core = line // 2, line % 2
    x, z = bus // RING, bus % RING
    up = ((y + 1) % RING) * 2 + core
    down = ((y + 3) % RING) * 2 + core
    sib = y * 2 + (1 - core)
    x1, x2, x3 = (x + 1) % RING, (x + 2) % RING, (x + 3) % RING
    z1, z2, z3 = (z + 1) % RING, (z + 2) % RING, (z + 3) % RING

    ids_copy = pltpu.make_async_copy(bus_hbm.at[pl.ds(bus * CHUNKS, CHUNKS)], ids, in_sem.at[0])
    ids_copy.start()
    val_copy = pltpu.make_async_copy(values_hbm, xa.at[pl.ds(0, SCEN_DEV)], in_sem.at[1])
    val_copy.start()

    barrier = pltpu.get_barrier_semaphore()
    for j in range(1, BUSES):
        pl.semaphore_signal(barrier, inc=1, device_id=(line, (bus + j) % BUSES), device_id_type=MESH)
    for other in (up, down, sib):
        pl.semaphore_signal(barrier, inc=1, device_id=(other, bus), device_id_type=MESH)

    def block_copy(zone, slot):
        return pltpu.make_async_copy(
            blocks_hbm.at[zone, slot], blk.at[zone, :, pl.ds(slot * ZB, ZB)], blk_sem.at[zone, slot]
        )

    def start_blocks(zone, _):
        for slot in range(SLOTS):
            block_copy(zone, slot).start()
        return 0

    lax.fori_loop(0, LZ, start_blocks, 0)

    inj0[ZONES] = jnp.zeros((HALF, ZB), BF16)
    inj1[ZONES] = jnp.zeros((HALF, ZB), BF16)
    wl[...] = jnp.zeros_like(wl)
    ids_copy.wait()
    bus_ids = ids[...]
    group = jnp.zeros_like(bus_ids)
    for g in range(1, BUSES):
        group = group + (bus_ids >= g * BUS_DEV).astype(jnp.int32)
    offset = bus_ids - group * BUS_DEV
    grp[...] = group.astype(F32)
    hi[...] = (offset >> 8).astype(F32)
    lo[...] = (offset & 255).astype(F32)

    sub16 = iota((16, 128), 0)

    def lanes(c, width=128):
        return pl.ds(pl.multiple_of(c * width, width), width)

    def mark(c, _):
        row = grp[pl.ds(c, 1), :]
        g01[pl.ds(pl.multiple_of(c * 16, 16), 16), :] = jnp.where(row == sub16, 1.0, 0.0).astype(BF16)
        digits = jnp.where(sub16 == 0, hi[pl.ds(c, 1), :], jnp.where(sub16 == 1, lo[pl.ds(c, 1), :], 0.0))
        xa[pl.ds(SCEN_DEV, 16), lanes(c)] = digits
        return 0

    lax.fori_loop(0, CHUNKS, mark, 0)
    ahead = lax.broadcasted_iota(jnp.int32, (128, 256), 0)
    place = lax.broadcasted_iota(jnp.int32, (128, 256), 1)
    steps = jnp.where((ahead <= place) | (place >= 128), 1.0, 0.0).astype(BF16)
    pre[...] = jnp.dot(g01[...], steps, preferred_element_type=F32)
    sub256 = iota((256, 128), 0)

    def rank(c, run):
        rows = pl.ds(pl.multiple_of(c * 16, 16), 16)
        counted = g01[rows, :].astype(F32) * (pre[rows, pl.ds(0, 128)] + run)
        position = jnp.sum(counted, axis=0, keepdims=True) - 1.0
        bt[:, lanes(c)] = jnp.where(position == sub256, 1.0, 0.0).astype(BF16)
        return run + pre[rows, pl.ds(128, 128)]

    lax.fori_loop(0, CHUNKS, rank, jnp.zeros((16, 128), F32))
    val_copy.wait()

    def exchange(j, owner):
        return pltpu.make_async_remote_copy(
            sv.at[j], rv.at[bus], xs_sem.at[j], xr_sem.at[bus],
            device_id=(line, owner), device_id_type=MESH,
        )

    pl.semaphore_wait(barrier, BUSES - 1 + 3)
    for batch in range(4):
        owners = [(bus + batch * 4 + i + 1) % BUSES for i in range(4)]
        owners_f = [o.astype(F32) for o in owners]

        def pick(c, _):
            row = grp[pl.ds(c, 1), :]
            vals = xa[:, lanes(c)]
            for i in range(4):
                lhs[pl.ds(i * ROWS, ROWS), lanes(c)] = jnp.where(row == owners_f[i], vals, 0.0).astype(BF16)
            return 0

        lax.fori_loop(0, CHUNKS, pick, 0)
        packed = lax.dot_general(
            lhs[pl.ds(0, 4 * ROWS), :], bt[...], NT, preferred_element_type=F32
        ).astype(BF16)
        for i in range(4):
            j = batch * 4 + i
            if j < BUSES - 1:
                sv[j] = packed[i * ROWS:(i + 1) * ROWS]
                exchange(j, owners[i]).start()
            else:
                rv[bus] = packed[i * ROWS:(i + 1) * ROWS]

    for j in range(1, BUSES):
        src = (bus + j) % BUSES
        pltpu.make_async_copy(rv.at[src], rv.at[src], xr_sem.at[src]).wait()

    sub256w = iota((256, 256), 0)

    def low_digit(k, _):
        row = rv[k, pl.ds(SCEN_DEV, 16), :].astype(F32)[1:2]
        bt[:, lanes(k, 256)] = jnp.where(row == sub256w, 1.0, 0.0).astype(BF16)
        return 0

    lax.fori_loop(0, BUSES, low_digit, 0)
    for part in range(3):

        def high_digit(k, _):
            vals = rv[k, pl.ds(0, SCEN_DEV), :].astype(F32)
            row = rv[k, pl.ds(SCEN_DEV, 16), :].astype(F32)[0:1]
            for i in range(6):
                lhs[pl.ds(i * SCEN_DEV, SCEN_DEV), lanes(k, 256)] = jnp.where(
                    row == float(part * 6 + i), vals, 0.0
                ).astype(BF16)
            return 0

        lax.fori_loop(0, BUSES, high_digit, 0)
        spread = lax.dot_general(
            lhs[...], bt[...], NT, preferred_element_type=F32
        ).astype(BF16)
        for i in range(6):
            for t in range(2):
                strip = 2 * (part * 6 + i) + t
                if strip >= ZONES * 5:
                    continue
                zone, lane = strip // 5, (strip % 5) * 128
                for s in range(4):
                    half, row = s % 2, (s // 2) * 16
                    dst = inj1 if half else inj0
                    dst[zone, pl.ds(pl.multiple_of(line * 32, 32) + row, 16), lane:lane + 128] = spread[
                        i * SCEN_DEV + s * 16:i * SCEN_DEV + s * 16 + 16, t * 128:t * 128 + 128
                    ]

    def gather(half, number, owner, first, count, target):
        buf = inj1 if half else inj0
        rows = buf.at[pl.ds(0, ZONES), pl.ds(pl.multiple_of(owner * 32, 32) + first, count)]
        return pltpu.make_async_remote_copy(
            rows, rows, gs_sem.at[half, number], gr_sem.at[half, number],
            device_id=(target, bus), device_id_type=MESH,
        )

    def arrival(half, number, owner, first, count):
        buf = inj1 if half else inj0
        rows = buf.at[pl.ds(0, ZONES), pl.ds(pl.multiple_of(owner * 32, 32) + first, count)]
        return pltpu.make_async_copy(rows, rows, gr_sem.at[half, number])

    far = ((y + 2) % RING) * 2 + core
    sib_up = ((y + 1) % RING) * 2 + (1 - core)
    sib_down = ((y + 3) % RING) * 2 + (1 - core)
    sib_far = ((y + 2) % RING) * 2 + (1 - core)

    ROUTES = (
        (line, 0, 32, up),
        (line, 0, 32, down),
        (line, 0, 32, sib),
        (down, 0, 16, up),
        (down, 0, 32, sib),
        (up, 16, 16, down),
        (up, 0, 32, sib),
        (far, 0, 16, sib),
        (far, 16, 16, sib),
    )

    def route(half, number):
        return gather(half, number, *ROUTES[number])

    def gather_start(half):
        for number in range(3):
            route(half, number).start()

    def gather_relay(half):
        arrival(half, 0, down, 0, 32).wait()
        route(half, 3).start()
        route(half, 4).start()
        arrival(half, 1, up, 0, 32).wait()
        route(half, 5).start()
        route(half, 6).start()

    def gather_last(half):
        arrival(half, 3, far, 0, 16).wait()
        route(half, 7).start()
        arrival(half, 5, far, 16, 16).wait()
        route(half, 8).start()

    def gather_finish(half):
        arrival(half, 2, sib, 0, 32).wait()
        arrival(half, 4, sib_down, 0, 32).wait()
        arrival(half, 6, sib_up, 0, 32).wait()
        arrival(half, 7, sib_far, 0, 16).wait()
        arrival(half, 8, sib_far, 16, 16).wait()

    gather_start(0)
    gather_relay(0)
    gather_start(1)
    gather_last(0)
    gather_finish(0)

    A, B = pl.ds(0, 256), pl.ds(256, 256)
    L, R = pl.ds(0, 128), pl.ds(128, 128)
    LO, HI = pl.ds(0, 2), pl.ds(2, 2)
    ALL = pl.ds(0, 4)

    def push(src, dst, t, step, device):
        pltpu.make_async_remote_copy(
            src, dst, fs_sem.at[t, step], fr_sem.at[t, step],
            device_id=(line, device), device_id_type=MESH,
        ).start()

    xp, xm, zp, zm = x1 * RING + z, x3 * RING + z, x * RING + z1, x * RING + z3

    def produce(t, zone, inj):
        for slot in range(SLOTS):
            @pl.when(t < LZ)
            def _():
                block_copy(zone, slot).wait()
        live = count_ref[zone, 0]
        pieces = []
        for slot in range(SLOTS):
            at = jnp.where(slot < live, zone_ref[zone, slot], ZONES)
            pieces.append(inj[at])
        out = lax.dot_general(
            jnp.concatenate(pieces, axis=1), blk[zone], NT, preferred_element_type=F32
        ).astype(BF16)
        flows[t] = out.reshape(RING, RING, 16, ZL)
        push(flows.at[t, x2, LO, :, A], ra.at[t, 0], t, 0, xp)
        push(flows.at[t, x2, HI, :, A], ra.at[t, 1], t, 0, xm)
        push(flows.at[t, LO, z2, :, B], ra.at[t, 2], t, 0, zp)
        push(flows.at[t, HI, z2, :, B], ra.at[t, 3], t, 0, zm)

    def arrived(buf, t, step):
        pltpu.make_async_copy(buf.at[t], buf.at[t], fr_sem.at[t, step]).wait()

    def add(a, b):
        return (a.astype(F32) + b.astype(F32)).astype(BF16)

    def first_b(t):
        arrived(ra, t, 0)
        flows[t, x1, LO, :, A] = add(flows[t, x1, LO, :, A], ra[t, 0])
        push(flows.at[t, x1, ALL, :, A], rb.at[t, 0], t, 1, xp)
        flows[t, x3, HI, :, A] = add(flows[t, x3, HI, :, A], ra[t, 1])
        push(flows.at[t, x3, ALL, :, A], rb.at[t, 1], t, 1, xm)
        flows[t, LO, z1, :, B] = add(flows[t, LO, z1, :, B], ra[t, 2])
        push(flows.at[t, ALL, z1, :, B], rb.at[t, 2], t, 1, zp)
        flows[t, HI, z3, :, B] = add(flows[t, HI, z3, :, B], ra[t, 3])
        push(flows.at[t, ALL, z3, :, B], rb.at[t, 3], t, 1, zm)

    def add3(a, b, c):
        return a.astype(F32) + b.astype(F32) + c.astype(F32)

    def second_a(t):
        arrived(rb, t, 1)
        sa[t, 0] = add3(flows[t, x, ALL, :, A], rb[t, 0], rb[t, 1]).astype(BF16)
        push(sa.at[t, 0, z2, :, L], rc.at[t, 0], t, 2, zp)
        push(sa.at[t, 0, z2, :, R], rc.at[t, 1], t, 2, zm)
        sa[t, 1] = add3(flows[t, ALL, z, :, B], rb[t, 2], rb[t, 3]).astype(BF16)
        push(sa.at[t, 1, x2, :, L], rc.at[t, 2], t, 2, xp)
        push(sa.at[t, 1, x2, :, R], rc.at[t, 3], t, 2, xm)

    def second_b(t):
        arrived(rc, t, 2)
        sa[t, 0, z1, :, L] = add(sa[t, 0, z1, :, L], rc[t, 0])
        push(sa.at[t, 0, z1], rd.at[t, 0], t, 3, zp)
        sa[t, 0, z3, :, R] = add(sa[t, 0, z3, :, R], rc[t, 1])
        push(sa.at[t, 0, z3], rd.at[t, 1], t, 3, zm)
        sa[t, 1, x1, :, L] = add(sa[t, 1, x1, :, L], rc[t, 2])
        push(sa.at[t, 1, x1], rd.at[t, 2], t, 3, xp)
        sa[t, 1, x3, :, R] = add(sa[t, 1, x3, :, R], rc[t, 3])
        push(sa.at[t, 1, x3], rd.at[t, 3], t, 3, xm)

    def finish(t, zone, half):
        arrived(rd, t, 3)
        ratings = jnp.concatenate([rating_ref[pl.ds(zone * 4 + i, 1), :] for i in range(4)], axis=1)
        flow = jnp.concatenate(
            [add3(sa[t, 0, z], rd[t, 0], rd[t, 1]), add3(sa[t, 1, x], rd[t, 2], rd[t, 3])], axis=1
        )
        loading = flow / ratings
        load_ref[pl.ds(pl.multiple_of(half * 16, 16), 16), lanes(zone, ZL)] = loading
        top = jnp.max(jnp.abs(loading), axis=0, keepdims=True)
        for i in range(4):
            row = pl.ds(zone * 4 + i, 1)
            wl[row, :] = jnp.maximum(wl[row, :], top[:, i * 128:(i + 1) * 128])
        for step, buf in enumerate((ra, rb, rc, rd)):
            pltpu.make_async_copy(buf.at[t], buf.at[t], fs_sem.at[t, step]).wait()

    parts = (pl.ds(0, WSPLIT * 4), pl.ds(WSPLIT * 4, 48 - WSPLIT * 4))

    def share(part):
        for j in range(1, BUSES):
            pltpu.make_async_remote_copy(
                wl.at[parts[part]], wr.at[bus, parts[part]], ws_sem.at[part, j], wr_sem.at[part, bus],
                device_id=(line, (bus + j) % BUSES), device_id_type=MESH,
            ).start()

    def stages(t):
        d1, d2, d3, d4 = LAG

        def when(lag, stage):
            @pl.when((t >= lag) & (t < T + lag))
            def _():
                stage(t - lag)

        when(d1, first_b)
        when(d2, second_a)
        when(d3, second_b)

        @pl.when((t >= d4) & (t < T + d4))
        def _():
            finish(t - d4, (t - d4) % LZ, (t - d4) // LZ)

        @pl.when(t == d4 + LZ + WSPLIT - 1)
        def _():
            share(0)

    def first_half(t, _):
        produce(t, t, inj0)

        @pl.when(t == 4)
        def _():
            gather_relay(1)

        @pl.when(t == 8)
        def _():
            gather_last(1)

        stages(t)
        return 0

    def second_half(t, _):
        produce(t, t - LZ, inj1)
        stages(t)
        return 0

    def drain(t, _):
        stages(t)
        return 0

    lax.fori_loop(0, LZ, first_half, 0)
    gather_finish(1)
    lax.fori_loop(LZ, T, second_half, 0)
    lax.fori_loop(T, T + LAG[3], drain, 0)

    share(1)
    for half in range(2):
        for number in range(len(ROUTES)):
            route(half, number).wait_send()
    for j in range(BUSES - 1):
        pltpu.make_async_copy(sv.at[j], sv.at[j], xs_sem.at[j]).wait()
    best = wl[...]
    for part in range(2):
        for j in range(1, BUSES):
            src = wr.at[(bus + j) % BUSES, parts[part]]
            pltpu.make_async_copy(src, src, wr_sem.at[part, (bus + j) % BUSES]).wait()
    for j in range(1, BUSES):
        best = jnp.maximum(best, wr[(bus + j) % BUSES])
    worst_ref[...] = best[0:LZ * 4]
    for part in range(2):
        for j in range(1, BUSES):
            src = wl.at[parts[part]]
            pltpu.make_async_copy(src, src, ws_sem.at[part, j]).wait()


def body(site_values, site_bus, block_count, block_zone, ptdf_blocks, rating):
    smem = pl.BlockSpec(memory_space=pltpu.SMEM)
    hbm = pl.BlockSpec(memory_space=pl.ANY)
    vmem = pl.BlockSpec(memory_space=pltpu.VMEM)
    dma = pltpu.SemaphoreType.DMA
    loading, worst = pl.pallas_call(
        kernel,
        out_shape=(
            jax.ShapeDtypeStruct((32, LZ * ZL), F32),
            jax.ShapeDtypeStruct((LZ * 4, 128), F32),
        ),
        in_specs=[smem, smem, hbm, hbm, hbm, vmem],
        out_specs=(vmem, vmem),
        scratch_shapes=[
            pltpu.VMEM((CHUNKS, 128), jnp.int32),
            pltpu.VMEM((CHUNKS, 128), F32),
            pltpu.VMEM((CHUNKS, 128), F32),
            pltpu.VMEM((CHUNKS, 128), F32),
            pltpu.VMEM((ROWS, SITE_DEV), F32),
            pltpu.VMEM((CHUNKS * 16, 128), BF16),
            pltpu.VMEM((CHUNKS * 16, 256), F32),
            pltpu.VMEM((256, SITE_DEV), BF16),
            pltpu.VMEM((384, SITE_DEV), BF16),
            pltpu.VMEM((BUSES - 1, ROWS, PER), BF16),
            pltpu.VMEM((BUSES, ROWS, PER), BF16),
            pltpu.VMEM((LZ, ZL, SLOTS * ZB), BF16),
            pltpu.VMEM((ZONES + 1, HALF, ZB), BF16),
            pltpu.VMEM((ZONES + 1, HALF, ZB), BF16),
            pltpu.VMEM((T, RING, RING, 16, ZL), BF16),
            pltpu.VMEM((T, 4, 2, 16, 256), BF16),
            pltpu.VMEM((T, 4, 4, 16, 256), BF16),
            pltpu.VMEM((T, 2, 4, 16, 256), BF16),
            pltpu.VMEM((T, 4, 16, 128), BF16),
            pltpu.VMEM((T, 4, 16, 256), BF16),
            pltpu.VMEM((48, 128), F32),
            pltpu.VMEM((BUSES, 48, 128), F32),
            dma((2,)),
            dma((LZ, SLOTS)),
            dma((BUSES,)),
            dma((BUSES,)),
            dma((2, 9)),
            dma((2, 9)),
            dma((T, 4)),
            dma((T, 4)),
            dma((2, BUSES)),
            dma((2, BUSES)),
        ],
        compiler_params=pltpu.CompilerParams(
            collective_id=0, has_side_effects=True, vmem_limit_bytes=62 * 1024 * 1024
        ),
        name="screen",
    )(
        block_count, block_zone, site_values, site_bus.reshape(-1, 128), ptdf_blocks,
        rating.reshape(-1, 128),
    )
    return loading, worst.reshape(-1)


def solution(mesh):
    return jax.shard_map(
        body,
        mesh=mesh,
        in_specs=(
            P("line", "bus"),
            P(),
            P("line", "bus"),
            P("line", "bus"),
            P("line", "bus", None, None),
            P("line"),
        ),
        out_specs=(P("bus", "line"), P("line")),
        check_vma=False,
    )
```

time: 637 us -> 111 us (0.17)
  waiting for transfers between devices: 236 us -> 0 us
  local copies, waits for them, and re-layouts: 112 us -> 6.06 us
  Pallas kernels: 0 us -> 104 us
  matrix products: 102 us -> 0 us
  loops' own time: 86.1 us -> 0 us
  blocking collectives: 72.1 us -> 0 us
  between operations: 13.9 us -> 0.64 us
  other arithmetic: 11.1 us -> 0 us
    unnamed x5 -> x0, waiting for transfers between devices: 202 us -> none
    pallas_call x0 -> x1, Pallas kernels: none -> 104 us  [body(): pl.pallas_call(kernel, out_shape=(jax.ShapeDtypeStruct((32, LZ * ZL), F32...]
    dot_general x49 -> x0, matrix products: 102 us -> none  [the longest x33 62.5 us: one_zone(): lax.dot_general(piece, block, (((1,), (1,)), ((), ())), preferred_element...]
    another operation x2 -> x0, loops' own time: 86.1 us -> none  [the longest x1 86.1 us: body(): lax.scan(one_zone, jnp.float32(0.0), (count_col, block_zone, ptdf_blocks))]
    pmax x1 -> x0, blocking collectives: 72.1 us -> none  [body(): worst = lax.pmax(local_worst, 'bus')]
    gather x4 -> x0, local copies, waits for them, and re-layouts: 39.3 us -> none  [the longest x2 23 us: body(): sorted_offsets = (jnp.take(own_ids, order) % bus_dev).astype(jnp.float32)]
    all_gather x1 -> x0, waiting for transfers between devices: 33.3 us -> none  [body(): injection = lax.all_gather(partial_value, 'line', axis=0, tiled=True)]
    unnamed x14 -> x4, local copies, waits for them, and re-layouts: 32.7 us -> 6.06 us
  transfers between devices with their start and end apart: 3 -> 0, of which waited for: 3 -> 0; matrix products, arithmetic and copies ran while one was open for 0% -> 0% of each run, Pallas kernels for 0% -> 0%
where the time goes in v1:
time: 111 us
  Pallas kernels  104 us (94%)
  local copies, waits for them, and re-layouts  6.06 us (5%)
    pallas_call x1, Pallas kernels, body(): pl.pallas_call(kernel, out_shape=(jax.ShapeDtypeStruct((32, LZ * ZL), F32...  104 us
    unnamed x4, local copies, waits for them, and re-layouts  6.06 us

profile of v1, /device:TPU:0, one launch (start us, length us, event | category | flops | bytes accessed | tf_op | source)
XLA Modules:
  0.0 110.8 jit_solution(1554853193622631835)
XLA Ops:
  0.6 1.3 %copy.8.count_ref = s32[11,1]{1,0:T(8,128)} copy(s32[11,1]{0,1:T(1,128)} %param.8) | data formatting | bytes 88 | tf_op args[2]
  2.0 1.4 %copy.9.zone_ref = s32[11,3]{1,0:T(8,128)} copy(s32[11,3]{0,1:T(4,128)} %param.9) | data formatting | bytes 264 | tf_op args[3]
  3.3 104.1 %screen.1 = (f32[32,5632]{1,0:T(8,128)}, f32[44,128]{1,0:T(8,128)}) custom-call(s32[11,1]{1,0:T(8,128)} %copy.8.count_ref, s32[11,3]{1,0:T(8,128)} %copy.9.zone_ref, f32[64,4096]{1,0:T(8,128)} %values_hbm.1, s32[512,128]{1,0:T(8,128)} %bitcast.3, bf16[11,3,512,640]{3,2,1,0:T(8,128)(2,1)} %blocks_hbm.1, f32[44,128]{1,0:T(8,128)} %bitcast.5), custom_call_target="tpu_custom_call" | custom-call | tf_op jit(solution)/shard_map/screen/pallas_call | solution.py:424
  107.4 2.0 %copy.12 = f32[32,5632]{1,0:T(8,128)} copy(f32[32,5632]{1,0:T(8,128)} %get-tuple-element.8) | data formatting | bytes 1441792
  109.4 1.3 %copy.13 = f32[5632]{0:T(1024)} copy(f32[5632]{0:T(1024)} %bitcast.4) | data formatting | bytes 45056

commit v2 on v1

--- a/solution.py
+++ b/solution.py
@@ -18,7 +18,9 @@
 SCEN_DEV = 64
 SITE_DEV = 4096
 PER = 256
-ROWS = 80
+ROWS = (48, 32)
+ROWS_ALL = 80
+DIGITS = 32
 CHUNKS = SITE_DEV // 128
 ZONES = 7
 ZB = 640
@@ -28,7 +30,7 @@
 HALF = 256
 T = 2 * LZ
 NT = (((1,), (1,)), ((), ()))
-LAG = (2, 4, 6, 8)
+LAG = (4, 8, 12, 16)
 WSPLIT = 8
 
 
@@ -37,9 +39,9 @@
 
 
 def kernel(
-    count_ref, zone_ref, values_hbm, bus_hbm, blocks_hbm, rating_ref,
+    count_hbm, zone_hbm, values_hbm, bus_hbm, blocks_hbm, rating_ref,
     load_ref, worst_ref,
-    ids, grp, hi, lo, xa, g01, pre, bt, lhs, sv, rv, blk, inj0, inj1,
+    live_ref, slot_ref, ids, grp, hi, lo, raw, xa, g01, pre, bt, lhs, sv0, sv1, rv0, rv1, blk, inj0, inj1,
     flows, ra, rb, sa, rc, rd, wl, wr,
     in_sem, blk_sem, xs_sem, xr_sem, gs_sem, gr_sem, fs_sem, fr_sem, ws_sem, wr_sem,
 ):
@@ -55,8 +57,18 @@
 
     ids_copy = pltpu.make_async_copy(bus_hbm.at[pl.ds(bus * CHUNKS, CHUNKS)], ids, in_sem.at[0])
     ids_copy.start()
-    val_copy = pltpu.make_async_copy(values_hbm, xa.at[pl.ds(0, SCEN_DEV)], in_sem.at[1])
-    val_copy.start()
+    val_copies = [
+        pltpu.make_async_copy(values_hbm.at[pl.ds(16 * q, 16)], raw.at[pl.ds(row, 16)], in_sem.at[1 + q])
+        for q, row in enumerate((0, 48, 16, 64))
+    ]
+    for copy in val_copies:
+        copy.start()
+    small_copies = [
+        pltpu.make_async_copy(count_hbm, live_ref, in_sem.at[5]),
+        pltpu.make_async_copy(zone_hbm, slot_ref, in_sem.at[6]),
+    ]
+    for copy in small_copies:
+        copy.start()
 
     barrier = pltpu.get_barrier_semaphore()
     for j in range(1, BUSES):
@@ -98,7 +110,7 @@
         row = grp[pl.ds(c, 1), :]
         g01[pl.ds(pl.multiple_of(c * 16, 16), 16), :] = jnp.where(row == sub16, 1.0, 0.0).astype(BF16)
         digits = jnp.where(sub16 == 0, hi[pl.ds(c, 1), :], jnp.where(sub16 == 1, lo[pl.ds(c, 1), :], 0.0))
-        xa[pl.ds(SCEN_DEV, 16), lanes(c)] = digits
+        xa[pl.ds(DIGITS, 16), lanes(c)] = digits.astype(BF16)
         return 0
 
     lax.fori_loop(0, CHUNKS, mark, 0)
@@ -116,77 +128,83 @@
         return run + pre[rows, pl.ds(128, 128)]
 
     lax.fori_loop(0, CHUNKS, rank, jnp.zeros((16, 128), F32))
-    val_copy.wait()
-
-    def exchange(j, owner):
-        return pltpu.make_async_remote_copy(
-            sv.at[j], rv.at[bus], xs_sem.at[j], xr_sem.at[bus],
-            device_id=(line, owner), device_id_type=MESH,
-        )
-
-    pl.semaphore_wait(barrier, BUSES - 1 + 3)
-    for batch in range(4):
-        owners = [(bus + batch * 4 + i + 1) % BUSES for i in range(4)]
-        owners_f = [o.astype(F32) for o in owners]
-
-        def pick(c, _):
-            row = grp[pl.ds(c, 1), :]
-            vals = xa[:, lanes(c)]
-            for i in range(4):
-                lhs[pl.ds(i * ROWS, ROWS), lanes(c)] = jnp.where(row == owners_f[i], vals, 0.0).astype(BF16)
-            return 0
-
-        lax.fori_loop(0, CHUNKS, pick, 0)
-        packed = lax.dot_general(
-            lhs[pl.ds(0, 4 * ROWS), :], bt[...], NT, preferred_element_type=F32
-        ).astype(BF16)
-        for i in range(4):
-            j = batch * 4 + i
-            if j < BUSES - 1:
-                sv[j] = packed[i * ROWS:(i + 1) * ROWS]
-                exchange(j, owners[i]).start()
-            else:
-                rv[bus] = packed[i * ROWS:(i + 1) * ROWS]
-
-    for j in range(1, BUSES):
-        src = (bus + j) % BUSES
-        pltpu.make_async_copy(rv.at[src], rv.at[src], xr_sem.at[src]).wait()
-
-    sub256w = iota((256, 256), 0)
+    for copy in val_copies:
+        copy.wait()
+
+    def narrow(c, _):
+        xa[pl.ds(0, 32), lanes(c)] = raw[pl.ds(0, 32), lanes(c)].astype(BF16)
+        xa[pl.ds(48, 32), lanes(c)] = raw[pl.ds(48, 32), lanes(c)].astype(BF16)
+        return 0
+
+    lax.fori_loop(0, CHUNKS, narrow, 0)
+
+    sv, rv = (sv0, sv1), (rv0, rv1)
+
+    def chosen(row, value, vals):
+        mask = jnp.where(jnp.broadcast_to(row, (16, row.shape[1])) == value, 1.0, 0.0).astype(BF16)
+        return vals * jnp.concatenate([mask] * (vals.shape[0] // 16), axis=0)
+
+    def pack(half):
+        rows = ROWS[half]
+        first = half * ROWS[0]
+        for batch in range(2):
+            owners = [(bus + batch * 8 + i + 1) % BUSES for i in range(8)]
+            owners_f = [o.astype(F32) for o in owners]
+
+            def pick(c, _):
+                row = grp[pl.ds(c, 1), :]
+                vals = xa[pl.ds(first, rows), lanes(c)]
+                for i in range(8):
+                    lhs[pl.ds(i * rows, rows), lanes(c)] = chosen(row, owners_f[i], vals)
+                return 0
+
+            lax.fori_loop(0, CHUNKS, pick, 0)
+            packed = lax.dot_general(
+                lhs[pl.ds(0, 8 * rows), :], bt[...], NT, preferred_element_type=F32
+            ).astype(BF16)
+            for i in range(8):
+                j = batch * 8 + i
+                if j < BUSES - 1:
+                    sv[half][j] = packed[i * rows:(i + 1) * rows]
+                    pltpu.make_async_remote_copy(
+                        sv[half].at[j], rv[half].at[bus], xs_sem.at[half, j], xr_sem.at[half, bus],
+                        device_id=(line, owners[i]), device_id_type=MESH,
+                    ).start()
+                else:
+                    rv[half][bus] = packed[i * rows:(i + 1) * rows]
+
+    def received(half):
+        for j in range(1, BUSES):
+            src = (bus + j) % BUSES
+            pltpu.make_async_copy(rv[half].at[src], rv[half].at[src], xr_sem.at[half, src]).wait()
 
     def low_digit(k, _):
-        row = rv[k, pl.ds(SCEN_DEV, 16), :].astype(F32)[1:2]
-        bt[:, lanes(k, 256)] = jnp.where(row == sub256w, 1.0, 0.0).astype(BF16)
-        return 0
-
-    lax.fori_loop(0, BUSES, low_digit, 0)
-    for part in range(3):
-
-        def high_digit(k, _):
-            vals = rv[k, pl.ds(0, SCEN_DEV), :].astype(F32)
-            row = rv[k, pl.ds(SCEN_DEV, 16), :].astype(F32)[0:1]
-            for i in range(6):
-                lhs[pl.ds(i * SCEN_DEV, SCEN_DEV), lanes(k, 256)] = jnp.where(
-                    row == float(part * 6 + i), vals, 0.0
-                ).astype(BF16)
-            return 0
-
-        lax.fori_loop(0, BUSES, high_digit, 0)
-        spread = lax.dot_general(
-            lhs[...], bt[...], NT, preferred_element_type=F32
-        ).astype(BF16)
-        for i in range(6):
-            for t in range(2):
-                strip = 2 * (part * 6 + i) + t
-                if strip >= ZONES * 5:
-                    continue
-                zone, lane = strip // 5, (strip % 5) * 128
-                for s in range(4):
-                    half, row = s % 2, (s // 2) * 16
-                    dst = inj1 if half else inj0
-                    dst[zone, pl.ds(pl.multiple_of(line * 32, 32) + row, 16), lane:lane + 128] = spread[
-                        i * SCEN_DEV + s * 16:i * SCEN_DEV + s * 16 + 16, t * 128:t * 128 + 128
-                    ]
+        row = rv0[k, pl.ds(DIGITS, 16), :].astype(F32)[1:2]
+        bt[:, lanes(k, 256)] = jnp.where(row == iota((256, 256), 0), 1.0, 0.0).astype(BF16)
+        return 0
+
+    def spread(half, inj):
+        for part in range(2):
+
+            def high_digit(k, _):
+                vals = rv[half][k, pl.ds(0, 32), :]
+                row = rv0[k, pl.ds(DIGITS, 16), :].astype(F32)[0:1]
+                for i in range(9):
+                    lhs[pl.ds(i * 32, 32), lanes(k, 256)] = chosen(row, float(part * 9 + i), vals)
+                return 0
+
+            lax.fori_loop(0, BUSES, high_digit, 0)
+            sums = lax.dot_general(
+                lhs[pl.ds(0, 288), :], bt[...], NT, preferred_element_type=F32
+            ).astype(BF16)
+            for i in range(9):
+                for t in range(2):
+                    strip = 2 * (part * 9 + i) + t
+                    if strip < ZONES * 5:
+                        zone, lane = strip // 5, (strip % 5) * 128
+                        inj[zone, pl.ds(pl.multiple_of(line * 32, 32), 32), lane:lane + 128] = sums[
+                            i * 32:(i + 1) * 32, t * 128:t * 128 + 128
+                        ]
 
     def gather(half, number, owner, first, count, target):
         buf = inj1 if half else inj0
@@ -246,11 +264,21 @@
         arrival(half, 7, sib_far, 0, 16).wait()
         arrival(half, 8, sib_far, 16, 16).wait()
 
+    pl.semaphore_wait(barrier, BUSES - 1 + 3)
+    pack(0)
+    pack(1)
+    received(0)
+    lax.fori_loop(0, BUSES, low_digit, 0)
+    spread(0, inj0)
     gather_start(0)
+    received(1)
+    spread(1, inj1)
     gather_relay(0)
     gather_start(1)
     gather_last(0)
     gather_finish(0)
+    for copy in small_copies:
+        copy.wait()
 
     A, B = pl.ds(0, 256), pl.ds(256, 256)
     L, R = pl.ds(0, 128), pl.ds(128, 128)
@@ -270,10 +298,10 @@
             @pl.when(t < LZ)
             def _():
                 block_copy(zone, slot).wait()
-        live = count_ref[zone, 0]
+        live = live_ref[0, zone]
         pieces = []
         for slot in range(SLOTS):
-            at = jnp.where(slot < live, zone_ref[zone, slot], ZONES)
+            at = jnp.where(slot < live, slot_ref[slot, zone], ZONES)
             pieces.append(inj[at])
         out = lax.dot_general(
             jnp.concatenate(pieces, axis=1), blk[zone], NT, preferred_element_type=F32
@@ -400,8 +428,8 @@
     for half in range(2):
         for number in range(len(ROUTES)):
             route(half, number).wait_send()
-    for j in range(BUSES - 1):
-        pltpu.make_async_copy(sv.at[j], sv.at[j], xs_sem.at[j]).wait()
+        for j in range(BUSES - 1):
+            pltpu.make_async_copy(sv[half].at[j], sv[half].at[j], xs_sem.at[half, j]).wait()
     best = wl[...]
     for part in range(2):
         for j in range(1, BUSES):
@@ -416,8 +444,12 @@
             pltpu.make_async_copy(src, src, ws_sem.at[part, j]).wait()
 
 
+def hand_over(load_in, worst_in, load_ref, worst_ref):
+    load_ref[...] = load_in[...]
+    worst_ref[...] = worst_in[...]
+
+
 def body(site_values, site_bus, block_count, block_zone, ptdf_blocks, rating):
-    smem = pl.BlockSpec(memory_space=pltpu.SMEM)
     hbm = pl.BlockSpec(memory_space=pl.ANY)
     vmem = pl.BlockSpec(memory_space=pltpu.VMEM)
     dma = pltpu.SemaphoreType.DMA
@@ -427,20 +459,25 @@
             jax.ShapeDtypeStruct((32, LZ * ZL), F32),
             jax.ShapeDtypeStruct((LZ * 4, 128), F32),
         ),
-        in_specs=[smem, smem, hbm, hbm, hbm, vmem],
+        in_specs=[hbm, hbm, hbm, hbm, hbm, vmem],
         out_specs=(vmem, vmem),
         scratch_shapes=[
+            pltpu.SMEM((1, LZ), jnp.int32),
+            pltpu.SMEM((SLOTS, LZ), jnp.int32),
             pltpu.VMEM((CHUNKS, 128), jnp.int32),
             pltpu.VMEM((CHUNKS, 128), F32),
             pltpu.VMEM((CHUNKS, 128), F32),
             pltpu.VMEM((CHUNKS, 128), F32),
-            pltpu.VMEM((ROWS, SITE_DEV), F32),
+            pltpu.VMEM((ROWS_ALL, SITE_DEV), F32),
+            pltpu.VMEM((ROWS_ALL, SITE_DEV), BF16),
             pltpu.VMEM((CHUNKS * 16, 128), BF16),
             pltpu.VMEM((CHUNKS * 16, 256), F32),
             pltpu.VMEM((256, SITE_DEV), BF16),
             pltpu.VMEM((384, SITE_DEV), BF16),
-            pltpu.VMEM((BUSES - 1, ROWS, PER), BF16),
-            pltpu.VMEM((BUSES, ROWS, PER), BF16),
+            pltpu.VMEM((BUSES - 1, ROWS[0], PER), BF16),
+            pltpu.VMEM((BUSES - 1, ROWS[1], PER), BF16),
+            pltpu.VMEM((BUSES, ROWS[0], PER), BF16),
+            pltpu.VMEM((BUSES, ROWS[1], PER), BF16),
             pltpu.VMEM((LZ, ZL, SLOTS * ZB), BF16),
             pltpu.VMEM((ZONES + 1, HALF, ZB), BF16),
             pltpu.VMEM((ZONES + 1, HALF, ZB), BF16),
@@ -452,10 +489,10 @@
             pltpu.VMEM((T, 4, 16, 256), BF16),
             pltpu.VMEM((48, 128), F32),
             pltpu.VMEM((BUSES, 48, 128), F32),
-            dma((2,)),
+            dma((7,)),
             dma((LZ, SLOTS)),
-            dma((BUSES,)),
-            dma((BUSES,)),
+            dma((2, BUSES)),
+            dma((2, BUSES)),
             dma((2, 9)),
             dma((2, 9)),
             dma((T, 4)),
@@ -468,9 +505,19 @@
         ),
         name="screen",
     )(
-        block_count, block_zone, site_values, site_bus.reshape(-1, 128), ptdf_blocks,
+        block_count.T, block_zone.T, site_values, site_bus.reshape(-1, 128), ptdf_blocks,
         rating.reshape(-1, 128),
     )
+    loading, worst = pl.pallas_call(
+        hand_over,
+        out_shape=(
+            jax.ShapeDtypeStruct((32, LZ * ZL), F32),
+            jax.ShapeDtypeStruct((LZ * 4, 128), F32),
+        ),
+        in_specs=[vmem, vmem],
+        out_specs=(vmem, vmem),
+        name="hand_over",
+    )(loading, worst)
     return loading, worst.reshape(-1)
 
 

time: 111 us -> 92.5 us (0.83)
  Pallas kernels: 104 us -> 91.6 us
  local copies, waits for them, and re-layouts: 6.06 us -> 0 us
    pallas_call x1, Pallas kernels: 104 us -> 89.6 us  [body(): pl.pallas_call(kernel, out_shape=(jax.ShapeDtypeStruct((32, LZ * ZL), F32...]
    unnamed x4 -> x0, local copies, waits for them, and re-layouts: 6.06 us -> none
    pallas_call x0 -> x1, Pallas kernels: none -> 2.02 us  [body(): pl.pallas_call(hand_over, out_shape=(jax.ShapeDtypeStruct((32, LZ * ZL),...]
where the time goes in v2:
time: 92.5 us; the launch traced here: 92.3 us
  Pallas kernels  91.6 us (99%)
    pallas_call x1, Pallas kernels, body(): pl.pallas_call(kernel, out_shape=(jax.ShapeDtypeStruct((32, LZ * ZL), F32...  89.6 us
    pallas_call x1, Pallas kernels, body(): pl.pallas_call(hand_over, out_shape=(jax.ShapeDtypeStruct((32, LZ * ZL),...  2.02 us

profile of v2, /device:TPU:0, one launch (start us, length us, event | category | flops | bytes accessed | tf_op | source)
XLA Modules:
  0.0 92.3 jit_solution(18191063878729375438)
XLA Ops:
  0.6 89.6 %screen.1 = (f32[32,5632]{1,0:T(8,128)}, f32[44,128]{1,0:T(8,128)}) custom-call(s32[1,11]{1,0:T(1,128)} %bitcast.8, s32[3,11]{1,0:T(4,128)} %bitcast.7, f32[64,4096]{1,0:T(8,128)} %values_hbm.1, s32[512,128]{1,0:T(8,128)} %bitcast.5, bf16[11,3,512,640]{3,2,1,0:T(8,128)(2,1)} %blocks_hbm.1, f32[44,128]{1,0:T(8,128)} %bitcast.6), custom_call_target="tpu_custom_call" | custom-call | tf_op jit(solution)/shard_map/screen/pallas_call | solution.py:456
  90.2 2.0 %hand_over.1 = (f32[32,5632]{1,0:T(8,128)}, f32[44,128]{1,0:T(8,128)}) custom-call(f32[32,5632]{1,0:T(8,128)} %get-tuple-element.6.load_in, f32[44,128]{1,0:T(8,128)} %get-tuple-element.7.worst_in), custom_call_target="tpu_custom_call" | custom-call | tf_op jit(solution)/shard_map/hand_over/pallas_call | solution.py:511

commit v3 on v2

--- a/solution.py
+++ b/solution.py
@@ -31,7 +31,8 @@
 T = 2 * LZ
 NT = (((1,), (1,)), ((), ()))
 LAG = (4, 8, 12, 16)
-WSPLIT = 8
+GATHERS = ((0, 0, 3), (0, 3, 4), (1, 0, 7))
+SHARES = (4, 8, 10, 12)
 
 
 def iota(shape, dim):
@@ -55,6 +56,12 @@
     x1, x2, x3 = (x + 1) % RING, (x + 2) % RING, (x + 3) % RING
     z1, z2, z3 = (z + 1) % RING, (z + 2) % RING, (z + 3) % RING
 
+    barrier = pltpu.get_barrier_semaphore()
+    for j in range(1, BUSES):
+        pl.semaphore_signal(barrier, inc=1, device_id=(line, (bus + j) % BUSES), device_id_type=MESH)
+    for other in (up, down, sib):
+        pl.semaphore_signal(barrier, inc=1, device_id=(other, bus), device_id_type=MESH)
+
     ids_copy = pltpu.make_async_copy(bus_hbm.at[pl.ds(bus * CHUNKS, CHUNKS)], ids, in_sem.at[0])
     ids_copy.start()
     val_copies = [
@@ -70,12 +77,6 @@
     for copy in small_copies:
         copy.start()
 
-    barrier = pltpu.get_barrier_semaphore()
-    for j in range(1, BUSES):
-        pl.semaphore_signal(barrier, inc=1, device_id=(line, (bus + j) % BUSES), device_id_type=MESH)
-    for other in (up, down, sib):
-        pl.semaphore_signal(barrier, inc=1, device_id=(other, bus), device_id_type=MESH)
-
     def block_copy(zone, slot):
         return pltpu.make_async_copy(
             blocks_hbm.at[zone, slot], blk.at[zone, :, pl.ds(slot * ZB, ZB)], blk_sem.at[zone, slot]
@@ -162,6 +163,8 @@
             packed = lax.dot_general(
                 lhs[pl.ds(0, 8 * rows), :], bt[...], NT, preferred_element_type=F32
             ).astype(BF16)
+            if half == 0 and batch == 0:
+                pl.semaphore_wait(barrier, BUSES - 1 + 3)
             for i in range(8):
                 j = batch * 8 + i
                 if j < BUSES - 1:
@@ -183,7 +186,7 @@
         bt[:, lanes(k, 256)] = jnp.where(row == iota((256, 256), 0), 1.0, 0.0).astype(BF16)
         return 0
 
-    def spread(half, inj):
+    def spread(half, inj, after):
         for part in range(2):
 
             def high_digit(k, _):
@@ -205,19 +208,23 @@
                         inj[zone, pl.ds(pl.multiple_of(line * 32, 32), 32), lane:lane + 128] = sums[
                             i * 32:(i + 1) * 32, t * 128:t * 128 + 128
                         ]
-
-    def gather(half, number, owner, first, count, target):
-        buf = inj1 if half else inj0
-        rows = buf.at[pl.ds(0, ZONES), pl.ds(pl.multiple_of(owner * 32, 32) + first, count)]
+            after[part]()
+
+    def gathered(step, owner, first, count):
+        half, zone, zones = GATHERS[step]
+        rows = pl.ds(pl.multiple_of(owner * 32, 32) + first, count)
+        return (inj1 if half else inj0).at[pl.ds(zone, zones), rows]
+
+    def gather(step, number, owner, first, count, target):
+        rows = gathered(step, owner, first, count)
         return pltpu.make_async_remote_copy(
-            rows, rows, gs_sem.at[half, number], gr_sem.at[half, number],
+            rows, rows, gs_sem.at[step, number], gr_sem.at[step, number],
             device_id=(target, bus), device_id_type=MESH,
         )
 
-    def arrival(half, number, owner, first, count):
-        buf = inj1 if half else inj0
-        rows = buf.at[pl.ds(0, ZONES), pl.ds(pl.multiple_of(owner * 32, 32) + first, count)]
-        return pltpu.make_async_copy(rows, rows, gr_sem.at[half, number])
+    def arrival(step, number, owner, first, count):
+        rows = gathered(step, owner, first, count)
+        return pltpu.make_async_copy(rows, rows, gr_sem.at[step, number])
 
     far = ((y + 2) % RING) * 2 + core
     sib_up = ((y + 1) % RING) * 2 + (1 - core)
@@ -236,47 +243,46 @@
         (far, 16, 16, sib),
     )
 
-    def route(half, number):
-        return gather(half, number, *ROUTES[number])
-
-    def gather_start(half):
+    def route(step, number):
+        return gather(step, number, *ROUTES[number])
+
+    def gather_start(step):
         for number in range(3):
-            route(half, number).start()
-
-    def gather_relay(half):
-        arrival(half, 0, down, 0, 32).wait()
-        route(half, 3).start()
-        route(half, 4).start()
-        arrival(half, 1, up, 0, 32).wait()
-        route(half, 5).start()
-        route(half, 6).start()
-
-    def gather_last(half):
-        arrival(half, 3, far, 0, 16).wait()
-        route(half, 7).start()
-        arrival(half, 5, far, 16, 16).wait()
-        route(half, 8).start()
-
-    def gather_finish(half):
-        arrival(half, 2, sib, 0, 32).wait()
-        arrival(half, 4, sib_down, 0, 32).wait()
-        arrival(half, 6, sib_up, 0, 32).wait()
-        arrival(half, 7, sib_far, 0, 16).wait()
-        arrival(half, 8, sib_far, 16, 16).wait()
-
-    pl.semaphore_wait(barrier, BUSES - 1 + 3)
+            route(step, number).start()
+
+    def gather_relay(step):
+        arrival(step, 0, down, 0, 32).wait()
+        route(step, 3).start()
+        route(step, 4).start()
+        arrival(step, 1, up, 0, 32).wait()
+        route(step, 5).start()
+        route(step, 6).start()
+
+    def gather_last(step):
+        arrival(step, 3, far, 0, 16).wait()
+        route(step, 7).start()
+        arrival(step, 5, far, 16, 16).wait()
+        route(step, 8).start()
+
+    def gather_finish(step):
+        arrival(step, 2, sib, 0, 32).wait()
+        arrival(step, 4, sib_down, 0, 32).wait()
+        arrival(step, 6, sib_up, 0, 32).wait()
+        arrival(step, 7, sib_far, 0, 16).wait()
+        arrival(step, 8, sib_far, 16, 16).wait()
+
     pack(0)
     pack(1)
     received(0)
     lax.fori_loop(0, BUSES, low_digit, 0)
-    spread(0, inj0)
-    gather_start(0)
+    spread(0, inj0, (lambda: gather_start(0), lambda: gather_start(1)))
     received(1)
-    spread(1, inj1)
-    gather_relay(0)
-    gather_start(1)
-    gather_last(0)
-    gather_finish(0)
+    spread(1, inj1, (lambda: gather_relay(0), lambda: gather_relay(1)))
+    gather_start(2)
+    for step in range(2):
+        gather_last(step)
+    for step in range(2):
+        gather_finish(step)
     for copy in small_copies:
         copy.wait()
 
@@ -320,13 +326,19 @@
 
     def first_b(t):
         arrived(ra, t, 0)
-        flows[t, x1, LO, :, A] = add(flows[t, x1, LO, :, A], ra[t, 0])
+        sums = (
+            add(flows[t, x1, LO, :, A], ra[t, 0]),
+            add(flows[t, x3, HI, :, A], ra[t, 1]),
+            add(flows[t, LO, z1, :, B], ra[t, 2]),
+            add(flows[t, HI, z3, :, B], ra[t, 3]),
+        )
+        flows[t, x1, LO, :, A] = sums[0]
+        flows[t, x3, HI, :, A] = sums[1]
+        flows[t, LO, z1, :, B] = sums[2]
+        flows[t, HI, z3, :, B] = sums[3]
         push(flows.at[t, x1, ALL, :, A], rb.at[t, 0], t, 1, xp)
-        flows[t, x3, HI, :, A] = add(flows[t, x3, HI, :, A], ra[t, 1])
         push(flows.at[t, x3, ALL, :, A], rb.at[t, 1], t, 1, xm)
-        flows[t, LO, z1, :, B] = add(flows[t, LO, z1, :, B], ra[t, 2])
         push(flows.at[t, ALL, z1, :, B], rb.at[t, 2], t, 1, zp)
-        flows[t, HI, z3, :, B] = add(flows[t, HI, z3, :, B], ra[t, 3])
         push(flows.at[t, ALL, z3, :, B], rb.at[t, 3], t, 1, zm)
 
     def add3(a, b, c):
@@ -334,22 +346,32 @@
 
     def second_a(t):
         arrived(rb, t, 1)
-        sa[t, 0] = add3(flows[t, x, ALL, :, A], rb[t, 0], rb[t, 1]).astype(BF16)
+        sums = (
+            add3(flows[t, x, ALL, :, A], rb[t, 0], rb[t, 1]).astype(BF16),
+            add3(flows[t, ALL, z, :, B], rb[t, 2], rb[t, 3]).astype(BF16),
+        )
+        sa[t, 0] = sums[0]
+        sa[t, 1] = sums[1]
         push(sa.at[t, 0, z2, :, L], rc.at[t, 0], t, 2, zp)
         push(sa.at[t, 0, z2, :, R], rc.at[t, 1], t, 2, zm)
-        sa[t, 1] = add3(flows[t, ALL, z, :, B], rb[t, 2], rb[t, 3]).astype(BF16)
         push(sa.at[t, 1, x2, :, L], rc.at[t, 2], t, 2, xp)
         push(sa.at[t, 1, x2, :, R], rc.at[t, 3], t, 2, xm)
 
     def second_b(t):
         arrived(rc, t, 2)
-        sa[t, 0, z1, :, L] = add(sa[t, 0, z1, :, L], rc[t, 0])
+        sums = (
+            add(sa[t, 0, z1, :, L], rc[t, 0]),
+            add(sa[t, 0, z3, :, R], rc[t, 1]),
+            add(sa[t, 1, x1, :, L], rc[t, 2]),
+            add(sa[t, 1, x3, :, R], rc[t, 3]),
+        )
+        sa[t, 0, z1, :, L] = sums[0]
+        sa[t, 0, z3, :, R] = sums[1]
+        sa[t, 1, x1, :, L] = sums[2]
+        sa[t, 1, x3, :, R] = sums[3]
         push(sa.at[t, 0, z1], rd.at[t, 0], t, 3, zp)
-        sa[t, 0, z3, :, R] = add(sa[t, 0, z3, :, R], rc[t, 1])
         push(sa.at[t, 0, z3], rd.at[t, 1], t, 3, zm)
-        sa[t, 1, x1, :, L] = add(sa[t, 1, x1, :, L], rc[t, 2])
         push(sa.at[t, 1, x1], rd.at[t, 2], t, 3, xp)
-        sa[t, 1, x3, :, R] = add(sa[t, 1, x3, :, R], rc[t, 3])
         push(sa.at[t, 1, x3], rd.at[t, 3], t, 3, xm)
 
     def finish(t, zone, half):
@@ -367,7 +389,7 @@
         for step, buf in enumerate((ra, rb, rc, rd)):
             pltpu.make_async_copy(buf.at[t], buf.at[t], fs_sem.at[t, step]).wait()
 
-    parts = (pl.ds(0, WSPLIT * 4), pl.ds(WSPLIT * 4, 48 - WSPLIT * 4))
+    parts = [pl.ds(first * 4, (last - first) * 4) for first, last in zip((0, *SHARES), SHARES)]
 
     def share(part):
         for j in range(1, BUSES):
@@ -392,20 +414,21 @@
         def _():
             finish(t - d4, (t - d4) % LZ, (t - d4) // LZ)
 
-        @pl.when(t == d4 + LZ + WSPLIT - 1)
-        def _():
-            share(0)
+        for part in range(len(parts) - 1):
+            @pl.when(t == d4 + LZ + SHARES[part] - 1)
+            def _(part=part):
+                share(part)
 
     def first_half(t, _):
         produce(t, t, inj0)
 
         @pl.when(t == 4)
         def _():
-            gather_relay(1)
+            gather_relay(2)
 
         @pl.when(t == 8)
         def _():
-            gather_last(1)
+            gather_last(2)
 
         stages(t)
         return 0
@@ -420,25 +443,26 @@
         return 0
 
     lax.fori_loop(0, LZ, first_half, 0)
-    gather_finish(1)
+    gather_finish(2)
     lax.fori_loop(LZ, T, second_half, 0)
     lax.fori_loop(T, T + LAG[3], drain, 0)
 
-    share(1)
+    share(len(parts) - 1)
+    for step in range(len(GATHERS)):
+        for number in range(len(ROUTES)):
+            route(step, number).wait_send()
     for half in range(2):
-        for number in range(len(ROUTES)):
-            route(half, number).wait_send()
         for j in range(BUSES - 1):
             pltpu.make_async_copy(sv[half].at[j], sv[half].at[j], xs_sem.at[half, j]).wait()
     best = wl[...]
-    for part in range(2):
+    for part in range(len(parts)):
         for j in range(1, BUSES):
             src = wr.at[(bus + j) % BUSES, parts[part]]
             pltpu.make_async_copy(src, src, wr_sem.at[part, (bus + j) % BUSES]).wait()
     for j in range(1, BUSES):
         best = jnp.maximum(best, wr[(bus + j) % BUSES])
     worst_ref[...] = best[0:LZ * 4]
-    for part in range(2):
+    for part in range(len(parts)):
         for j in range(1, BUSES):
             src = wl.at[parts[part]]
             pltpu.make_async_copy(src, src, ws_sem.at[part, j]).wait()
@@ -493,12 +517,12 @@
             dma((LZ, SLOTS)),
             dma((2, BUSES)),
             dma((2, BUSES)),
-            dma((2, 9)),
-            dma((2, 9)),
+            dma((len(GATHERS), 9)),
+            dma((len(GATHERS), 9)),
             dma((T, 4)),
             dma((T, 4)),
-            dma((2, BUSES)),
-            dma((2, BUSES)),
+            dma((len(SHARES), BUSES)),
+            dma((len(SHARES), BUSES)),
         ],
         compiler_params=pltpu.CompilerParams(
             collective_id=0, has_side_effects=True, vmem_limit_bytes=62 * 1024 * 1024

time: 92.5 us -> 88.7 us (0.959)
  Pallas kernels: 91.6 us -> 87.9 us
    pallas_call x1, Pallas kernels: 89.6 us -> 85.9 us  [body(): pl.pallas_call(kernel, out_shape=(jax.ShapeDtypeStruct((32, LZ * ZL), F32...]
where the time goes in v3:
time: 88.7 us; the launch traced here: 88.5 us
  Pallas kernels  87.9 us (99%)
    pallas_call x1, Pallas kernels, body(): pl.pallas_call(kernel, out_shape=(jax.ShapeDtypeStruct((32, LZ * ZL), F32...  85.9 us
    pallas_call x1, Pallas kernels, body(): pl.pallas_call(hand_over, out_shape=(jax.ShapeDtypeStruct((32, LZ * ZL),...  2.02 us

profile of v3, /device:TPU:0, one launch (start us, length us, event | category | flops | bytes accessed | tf_op | source)
XLA Modules:
  0.0 88.5 jit_solution(14153997388550441300)
XLA Ops:
  0.6 85.9 %screen.1 = (f32[32,5632]{1,0:T(8,128)}, f32[44,128]{1,0:T(8,128)}) custom-call(s32[1,11]{1,0:T(1,128)} %bitcast.8, s32[3,11]{1,0:T(4,128)} %bitcast.7, f32[64,4096]{1,0:T(8,128)} %values_hbm.1, s32[512,128]{1,0:T(8,128)} %bitcast.5, bf16[11,3,512,640]{3,2,1,0:T(8,128)(2,1)} %blocks_hbm.1, f32[44,128]{1,0:T(8,128)} %bitcast.6), custom_call_target="tpu_custom_call" | custom-call | tf_op jit(solution)/shard_map/screen/pallas_call | solution.py:480
  86.5 2.0 %hand_over.1 = (f32[32,5632]{1,0:T(8,128)}, f32[44,128]{1,0:T(8,128)}) custom-call(f32[32,5632]{1,0:T(8,128)} %get-tuple-element.6.load_in, f32[44,128]{1,0:T(8,128)} %get-tuple-element.7.worst_in), custom_call_target="tpu_custom_call" | custom-call | tf_op jit(solution)/shard_map/hand_over/pallas_call | solution.py:535

commit v4 on v3

--- a/solution.py
+++ b/solution.py
@@ -29,10 +29,13 @@
 SLOTS = 3
 HALF = 256
 T = 2 * LZ
+DIRECT = 2
+TR = T - DIRECT
 NT = (((1,), (1,)), ((), ()))
 LAG = (4, 8, 12, 16)
+GATHER_AT = (4, 8)
 GATHERS = ((0, 0, 3), (0, 3, 4), (1, 0, 7))
-SHARES = (4, 8, 10, 12)
+SHARES = (4, 8, 12)
 
 
 def iota(shape, dim):
@@ -43,8 +46,8 @@
     count_hbm, zone_hbm, values_hbm, bus_hbm, blocks_hbm, rating_ref,
     load_ref, worst_ref,
     live_ref, slot_ref, ids, grp, hi, lo, raw, xa, g01, pre, bt, lhs, sv0, sv1, rv0, rv1, blk, inj0, inj1,
-    flows, ra, rb, sa, rc, rd, wl, wr,
-    in_sem, blk_sem, xs_sem, xr_sem, gs_sem, gr_sem, fs_sem, fr_sem, ws_sem, wr_sem,
+    flows, ra, rb, sa, rc, rd, rs, wl, wr,
+    in_sem, blk_sem, xs_sem, xr_sem, gs_sem, gr_sem, fs_sem, fr_sem, ds_sem, dr_sem, ws_sem, wr_sem,
 ):
     line = lax.axis_index("line")
     bus = lax.axis_index("bus")
@@ -299,11 +302,16 @@
 
     xp, xm, zp, zm = x1 * RING + z, x3 * RING + z, x * RING + z1, x * RING + z3
 
+    def add(a, b):
+        return (a.astype(F32) + b.astype(F32)).astype(BF16)
+
+    def add3(a, b, c):
+        return a.astype(F32) + b.astype(F32) + c.astype(F32)
+
+    def arrived(buf, t, step):
+        pltpu.make_async_copy(buf.at[t], buf.at[t], fr_sem.at[t, step]).wait()
+
     def produce(t, zone, inj):
-        for slot in range(SLOTS):
-            @pl.when(t < LZ)
-            def _():
-                block_copy(zone, slot).wait()
         live = live_ref[0, zone]
         pieces = []
         for slot in range(SLOTS):
@@ -312,82 +320,105 @@
         out = lax.dot_general(
             jnp.concatenate(pieces, axis=1), blk[zone], NT, preferred_element_type=F32
         ).astype(BF16)
-        flows[t] = out.reshape(RING, RING, 16, ZL)
-        push(flows.at[t, x2, LO, :, A], ra.at[t, 0], t, 0, xp)
-        push(flows.at[t, x2, HI, :, A], ra.at[t, 1], t, 0, xm)
-        push(flows.at[t, LO, z2, :, B], ra.at[t, 2], t, 0, zp)
-        push(flows.at[t, HI, z2, :, B], ra.at[t, 3], t, 0, zm)
-
-    def arrived(buf, t, step):
-        pltpu.make_async_copy(buf.at[t], buf.at[t], fr_sem.at[t, step]).wait()
-
-    def add(a, b):
-        return (a.astype(F32) + b.astype(F32)).astype(BF16)
+
+        def store():
+            flows[t] = out.reshape(RING, RING, 16, ZL)
+
+        def send():
+            push(flows.at[t, x2, LO, :, A], ra.at[t, 0], t, 0, xp)
+            push(flows.at[t, x2, HI, :, A], ra.at[t, 1], t, 0, xm)
+            push(flows.at[t, LO, z2, :, B], ra.at[t, 2], t, 0, zp)
+            push(flows.at[t, HI, z2, :, B], ra.at[t, 3], t, 0, zm)
+
+        return store, send
 
     def first_b(t):
-        arrived(ra, t, 0)
         sums = (
             add(flows[t, x1, LO, :, A], ra[t, 0]),
             add(flows[t, x3, HI, :, A], ra[t, 1]),
             add(flows[t, LO, z1, :, B], ra[t, 2]),
             add(flows[t, HI, z3, :, B], ra[t, 3]),
         )
-        flows[t, x1, LO, :, A] = sums[0]
-        flows[t, x3, HI, :, A] = sums[1]
-        flows[t, LO, z1, :, B] = sums[2]
-        flows[t, HI, z3, :, B] = sums[3]
-        push(flows.at[t, x1, ALL, :, A], rb.at[t, 0], t, 1, xp)
-        push(flows.at[t, x3, ALL, :, A], rb.at[t, 1], t, 1, xm)
-        push(flows.at[t, ALL, z1, :, B], rb.at[t, 2], t, 1, zp)
-        push(flows.at[t, ALL, z3, :, B], rb.at[t, 3], t, 1, zm)
-
-    def add3(a, b, c):
-        return a.astype(F32) + b.astype(F32) + c.astype(F32)
+
+        def store():
+            flows[t, x1, LO, :, A] = sums[0]
+            flows[t, x3, HI, :, A] = sums[1]
+            flows[t, LO, z1, :, B] = sums[2]
+            flows[t, HI, z3, :, B] = sums[3]
+
+        def send():
+            push(flows.at[t, x1, ALL, :, A], rb.at[t, 0], t, 1, xp)
+            push(flows.at[t, x3, ALL, :, A], rb.at[t, 1], t, 1, xm)
+            push(flows.at[t, ALL, z1, :, B], rb.at[t, 2], t, 1, zp)
+            push(flows.at[t, ALL, z3, :, B], rb.at[t, 3], t, 1, zm)
+
+        return store, send
 
     def second_a(t):
-        arrived(rb, t, 1)
         sums = (
             add3(flows[t, x, ALL, :, A], rb[t, 0], rb[t, 1]).astype(BF16),
             add3(flows[t, ALL, z, :, B], rb[t, 2], rb[t, 3]).astype(BF16),
         )
-        sa[t, 0] = sums[0]
-        sa[t, 1] = sums[1]
-        push(sa.at[t, 0, z2, :, L], rc.at[t, 0], t, 2, zp)
-        push(sa.at[t, 0, z2, :, R], rc.at[t, 1], t, 2, zm)
-        push(sa.at[t, 1, x2, :, L], rc.at[t, 2], t, 2, xp)
-        push(sa.at[t, 1, x2, :, R], rc.at[t, 3], t, 2, xm)
+
+        def store():
+            sa[t, 0] = sums[0]
+            sa[t, 1] = sums[1]
+
+        def send():
+            push(sa.at[t, 0, z2, :, L], rc.at[t, 0], t, 2, zp)
+            push(sa.at[t, 0, z2, :, R], rc.at[t, 1], t, 2, zm)
+            push(sa.at[t, 1, x2, :, L], rc.at[t, 2], t, 2, xp)
+            push(sa.at[t, 1, x2, :, R], rc.at[t, 3], t, 2, xm)
+
+        return store, send
 
     def second_b(t):
-        arrived(rc, t, 2)
         sums = (
             add(sa[t, 0, z1, :, L], rc[t, 0]),
             add(sa[t, 0, z3, :, R], rc[t, 1]),
             add(sa[t, 1, x1, :, L], rc[t, 2]),
             add(sa[t, 1, x3, :, R], rc[t, 3]),
         )
-        sa[t, 0, z1, :, L] = sums[0]
-        sa[t, 0, z3, :, R] = sums[1]
-        sa[t, 1, x1, :, L] = sums[2]
-        sa[t, 1, x3, :, R] = sums[3]
-        push(sa.at[t, 0, z1], rd.at[t, 0], t, 3, zp)
-        push(sa.at[t, 0, z3], rd.at[t, 1], t, 3, zm)
-        push(sa.at[t, 1, x1], rd.at[t, 2], t, 3, xp)
-        push(sa.at[t, 1, x3], rd.at[t, 3], t, 3, xm)
-
-    def finish(t, zone, half):
-        arrived(rd, t, 3)
+
+        def store():
+            sa[t, 0, z1, :, L] = sums[0]
+            sa[t, 0, z3, :, R] = sums[1]
+            sa[t, 1, x1, :, L] = sums[2]
+            sa[t, 1, x3, :, R] = sums[3]
+
+        def send():
+            push(sa.at[t, 0, z1], rd.at[t, 0], t, 3, zp)
+            push(sa.at[t, 0, z3], rd.at[t, 1], t, 3, zm)
+            push(sa.at[t, 1, x1], rd.at[t, 2], t, 3, xp)
+            push(sa.at[t, 1, x3], rd.at[t, 3], t, 3, xm)
+
+        return store, send
+
+    def settle(t, flow):
+        zone, half = t % LZ, t // LZ
         ratings = jnp.concatenate([rating_ref[pl.ds(zone * 4 + i, 1), :] for i in range(4)], axis=1)
+        loading = flow / ratings
+        top = jnp.max(jnp.abs(loading), axis=0, keepdims=True)
+        start = half * 16 if isinstance(half, int) else pl.multiple_of(half * 16, 16)
+        left = zone * ZL if isinstance(zone, int) else pl.multiple_of(zone * ZL, ZL)
+        load_ref[pl.ds(start, 16), pl.ds(left, ZL)] = loading
+        for i in range(4):
+            row = pl.ds(zone * 4 + i, 1)
+            wl[row, :] = jnp.maximum(wl[row, :], top[:, i * 128:(i + 1) * 128])
+
+    def finish(t):
         flow = jnp.concatenate(
             [add3(sa[t, 0, z], rd[t, 0], rd[t, 1]), add3(sa[t, 1, x], rd[t, 2], rd[t, 3])], axis=1
         )
-        loading = flow / ratings
-        load_ref[pl.ds(pl.multiple_of(half * 16, 16), 16), lanes(zone, ZL)] = loading
-        top = jnp.max(jnp.abs(loading), axis=0, keepdims=True)
-        for i in range(4):
-            row = pl.ds(zone * 4 + i, 1)
-            wl[row, :] = jnp.maximum(wl[row, :], top[:, i * 128:(i + 1) * 128])
-        for step, buf in enumerate((ra, rb, rc, rd)):
-            pltpu.make_async_copy(buf.at[t], buf.at[t], fs_sem.at[t, step]).wait()
+
+        def store():
+            settle(t, flow)
+
+        def send():
+            for step, buf in enumerate((ra, rb, rc, rd)):
+                pltpu.make_async_copy(buf.at[t], buf.at[t], fs_sem.at[t, step]).wait()
+
+        return store, send
 
     parts = [pl.ds(first * 4, (last - first) * 4) for first, last in zip((0, *SHARES), SHARES)]
 
@@ -398,56 +429,65 @@
                 device_id=(line, (bus + j) % BUSES), device_id_type=MESH,
             ).start()
 
-    def stages(t):
-        d1, d2, d3, d4 = LAG
-
-        def when(lag, stage):
-            @pl.when((t >= lag) & (t < T + lag))
-            def _():
-                stage(t - lag)
-
-        when(d1, first_b)
-        when(d2, second_a)
-        when(d3, second_b)
-
-        @pl.when((t >= d4) & (t < T + d4))
-        def _():
-            finish(t - d4, (t - d4) % LZ, (t - d4) // LZ)
-
-        for part in range(len(parts) - 1):
-            @pl.when(t == d4 + LZ + SHARES[part] - 1)
-            def _(part=part):
-                share(part)
-
-    def first_half(t, _):
-        produce(t, t, inj0)
-
-        @pl.when(t == 4)
-        def _():
-            gather_relay(2)
-
-        @pl.when(t == 8)
-        def _():
-            gather_last(2)
-
-        stages(t)
-        return 0
-
-    def second_half(t, _):
-        produce(t, t - LZ, inj1)
-        stages(t)
-        return 0
-
-    def drain(t, _):
-        stages(t)
-        return 0
-
-    lax.fori_loop(0, LZ, first_half, 0)
-    gather_finish(2)
-    lax.fori_loop(LZ, T, second_half, 0)
-    lax.fori_loop(T, T + LAG[3], drain, 0)
+    STEPS = tuple(zip((first_b, second_a, second_b, finish), (ra, rb, rc, rd), LAG))
+
+    def straight(t):
+        for j in range(1, BUSES):
+            owner = (bus + j) % BUSES
+            pltpu.make_async_remote_copy(
+                flows.at[t, owner // RING, owner % RING], rs.at[t - TR, bus], ds_sem.at[t - TR, j], dr_sem.at[t - TR, bus],
+                device_id=(line, owner), device_id_type=MESH,
+            ).start()
+
+    def straight_finish(t):
+        flow = flows[t, x, z].astype(F32)
+        for j in range(1, BUSES):
+            src = rs.at[t - TR, (bus + j) % BUSES]
+            pltpu.make_async_copy(src, src, dr_sem.at[t - TR, (bus + j) % BUSES]).wait()
+        for j in range(1, BUSES):
+            flow = flow + rs[t - TR, (bus + j) % BUSES].astype(F32)
+        settle(t, flow)
+
+    def iteration(active, produces, t):
+        if produces:
+            if produces == 1:
+                for slot in range(SLOTS):
+                    block_copy(t, slot).wait()
+            store, send = produce(t, t % LZ, inj0 if produces == 1 else inj1)
+            store()
+            if produces == 3:
+                straight(t)
+            else:
+                send()
+        for step in active:
+            arrived(STEPS[step][1], t - STEPS[step][2], step)
+            store, send = STEPS[step][0](t - STEPS[step][2])
+            store()
+            send()
+
+    before = {GATHER_AT[0]: [lambda: gather_relay(2)], GATHER_AT[1]: [lambda: gather_last(2)], LZ: [lambda: gather_finish(2)]}
+    for part in range(len(parts) - 1):
+        before.setdefault(LAG[3] + LZ + SHARES[part], []).append(functools.partial(share, part))
+    for t in range(TR, T):
+        before.setdefault(TR + LAG[3] - 1, []).append(functools.partial(straight_finish, t))
+    edges = sorted({0, LZ, TR, T, TR + LAG[3], *LAG, *(TR + lag for lag in LAG), *before})
+    for first, last in zip(edges, edges[1:]):
+        for hook in before.get(first, ()):
+            hook()
+        active = [step for step in range(4) if LAG[step] <= first < TR + LAG[step]]
+        produces = 0 if first >= T else 3 if first >= TR else 2 if first >= LZ else 1
+
+        def run(t, _, active=active, produces=produces):
+            iteration(active, produces, t)
+            return 0
+
+        lax.fori_loop(first, last, run, 0)
 
     share(len(parts) - 1)
+    for t in range(TR, T):
+        for j in range(1, BUSES):
+            src = rs.at[t - TR, 0]
+            pltpu.make_async_copy(src, src, ds_sem.at[t - TR, j]).wait()
     for step in range(len(GATHERS)):
         for number in range(len(ROUTES)):
             route(step, number).wait_send()
@@ -506,11 +546,12 @@
             pltpu.VMEM((ZONES + 1, HALF, ZB), BF16),
             pltpu.VMEM((ZONES + 1, HALF, ZB), BF16),
             pltpu.VMEM((T, RING, RING, 16, ZL), BF16),
-            pltpu.VMEM((T, 4, 2, 16, 256), BF16),
-            pltpu.VMEM((T, 4, 4, 16, 256), BF16),
-            pltpu.VMEM((T, 2, 4, 16, 256), BF16),
-            pltpu.VMEM((T, 4, 16, 128), BF16),
-            pltpu.VMEM((T, 4, 16, 256), BF16),
+            pltpu.VMEM((TR, 4, 2, 16, 256), BF16),
+            pltpu.VMEM((TR, 4, 4, 16, 256), BF16),
+            pltpu.VMEM((TR, 2, 4, 16, 256), BF16),
+            pltpu.VMEM((TR, 4, 16, 128), BF16),
+            pltpu.VMEM((TR, 4, 16, 256), BF16),
+            pltpu.VMEM((DIRECT, BUSES, 16, ZL), BF16),
             pltpu.VMEM((48, 128), F32),
             pltpu.VMEM((BUSES, 48, 128), F32),
             dma((7,)),
@@ -519,8 +560,10 @@
             dma((2, BUSES)),
             dma((len(GATHERS), 9)),
             dma((len(GATHERS), 9)),
-            dma((T, 4)),
-            dma((T, 4)),
+            dma((TR, 4)),
+            dma((TR, 4)),
+            dma((DIRECT, BUSES)),
+            dma((DIRECT, BUSES)),
             dma((len(SHARES), BUSES)),
             dma((len(SHARES), BUSES)),
         ],

time: 88.7 us -> 92.4 us (1.042)
  Pallas kernels: 87.9 us -> 91.6 us
    pallas_call x1, Pallas kernels: 85.9 us -> 89.5 us  [body(): pl.pallas_call(kernel, out_shape=(jax.ShapeDtypeStruct((32, LZ * ZL), F32...]
where the time goes in v4:
time: 92.4 us; the launch traced here: 92.2 us
  Pallas kernels  91.6 us (99%)
    pallas_call x1, Pallas kernels, body(): pl.pallas_call(kernel, out_shape=(jax.ShapeDtypeStruct((32, LZ * ZL), F32...  89.5 us
    pallas_call x1, Pallas kernels, body(): pl.pallas_call(hand_over, out_shape=(jax.ShapeDtypeStruct((32, LZ * ZL),...  2.02 us

profile of v4, /device:TPU:0, one launch (start us, length us, event | category | flops | bytes accessed | tf_op | source)
XLA Modules:
  0.0 92.2 jit_solution(6939041410863329041)
XLA Ops:
  0.6 89.5 %screen.1 = (f32[32,5632]{1,0:T(8,128)}, f32[44,128]{1,0:T(8,128)}) custom-call(s32[1,11]{1,0:T(1,128)} %bitcast.8, s32[3,11]{1,0:T(4,128)} %bitcast.7, f32[64,4096]{1,0:T(8,128)} %values_hbm.1, s32[512,128]{1,0:T(8,128)} %bitcast.5, bf16[11,3,512,640]{3,2,1,0:T(8,128)(2,1)} %blocks_hbm.1, f32[44,128]{1,0:T(8,128)} %bitcast.6), custom_call_target="tpu_custom_call" | custom-call | tf_op jit(solution)/shard_map/screen/pallas_call | solution.py:520
  90.2 2.0 %hand_over.1 = (f32[32,5632]{1,0:T(8,128)}, f32[44,128]{1,0:T(8,128)}) custom-call(f32[32,5632]{1,0:T(8,128)} %get-tuple-element.6.load_in, f32[44,128]{1,0:T(8,128)} %get-tuple-element.7.worst_in), custom_call_target="tpu_custom_call" | custom-call | tf_op jit(solution)/shard_map/hand_over/pallas_call | solution.py:578

commit v5 on v3

--- a/solution.py
+++ b/solution.py
@@ -31,7 +31,7 @@
 T = 2 * LZ
 NT = (((1,), (1,)), ((), ()))
 LAG = (4, 8, 12, 16)
-GATHERS = ((0, 0, 3), (0, 3, 4), (1, 0, 7))
+GATHERS = ((0, 0, 3), (0, 3, 2), (0, 5, 1), (0, 6, 1), (1, 0, 7))
 SHARES = (4, 8, 10, 12)
 
 
@@ -41,10 +41,10 @@
 
 def kernel(
     count_hbm, zone_hbm, values_hbm, bus_hbm, blocks_hbm, rating_ref,
-    load_ref, worst_ref,
+    load_hbm, worst_ref,
     live_ref, slot_ref, ids, grp, hi, lo, raw, xa, g01, pre, bt, lhs, sv0, sv1, rv0, rv1, blk, inj0, inj1,
-    flows, ra, rb, sa, rc, rd, wl, wr,
-    in_sem, blk_sem, xs_sem, xr_sem, gs_sem, gr_sem, fs_sem, fr_sem, ws_sem, wr_sem,
+    flows, ra, rb, sa, rc, rd, load_ref, wl, wr,
+    in_sem, blk_sem, xs_sem, xr_sem, gs_sem, gr_sem, fs_sem, fr_sem, ws_sem, wr_sem, out_sem,
 ):
     line = lax.axis_index("line")
     bus = lax.axis_index("bus")
@@ -275,14 +275,19 @@
     pack(1)
     received(0)
     lax.fori_loop(0, BUSES, low_digit, 0)
-    spread(0, inj0, (lambda: gather_start(0), lambda: gather_start(1)))
+    early = range(1, len(GATHERS) - 1)
+    late = len(GATHERS) - 1
+
+    def each(stage, steps):
+        for step in steps:
+            stage(step)
+
+    spread(0, inj0, (lambda: gather_start(0), lambda: each(gather_start, early)))
     received(1)
-    spread(1, inj1, (lambda: gather_relay(0), lambda: gather_relay(1)))
-    gather_start(2)
-    for step in range(2):
-        gather_last(step)
-    for step in range(2):
-        gather_finish(step)
+    spread(1, inj1, (lambda: gather_relay(0), lambda: each(gather_relay, early)))
+    gather_start(late)
+    each(gather_last, range(late))
+    each(gather_finish, range(late))
     for copy in small_copies:
         copy.wait()
 
@@ -374,6 +379,10 @@
         push(sa.at[t, 1, x1], rd.at[t, 2], t, 3, xp)
         push(sa.at[t, 1, x3], rd.at[t, 3], t, 3, xm)
 
+    def leave(t, zone, half):
+        part = (pl.ds(pl.multiple_of(half * 16, 16), 16), lanes(zone, ZL))
+        return pltpu.make_async_copy(load_ref.at[part], load_hbm.at[part], out_sem.at[t])
+
     def finish(t, zone, half):
         arrived(rd, t, 3)
         ratings = jnp.concatenate([rating_ref[pl.ds(zone * 4 + i, 1), :] for i in range(4)], axis=1)
@@ -382,6 +391,7 @@
         )
         loading = flow / ratings
         load_ref[pl.ds(pl.multiple_of(half * 16, 16), 16), lanes(zone, ZL)] = loading
+        leave(t, zone, half).start()
         top = jnp.max(jnp.abs(loading), axis=0, keepdims=True)
         for i in range(4):
             row = pl.ds(zone * 4 + i, 1)
@@ -424,11 +434,11 @@
 
         @pl.when(t == 4)
         def _():
-            gather_relay(2)
+            gather_relay(late)
 
         @pl.when(t == 8)
         def _():
-            gather_last(2)
+            gather_last(late)
 
         stages(t)
         return 0
@@ -443,7 +453,7 @@
         return 0
 
     lax.fori_loop(0, LZ, first_half, 0)
-    gather_finish(2)
+    gather_finish(late)
     lax.fori_loop(LZ, T, second_half, 0)
     lax.fori_loop(T, T + LAG[3], drain, 0)
 
@@ -454,6 +464,12 @@
     for half in range(2):
         for j in range(BUSES - 1):
             pltpu.make_async_copy(sv[half].at[j], sv[half].at[j], xs_sem.at[half, j]).wait()
+
+    def gone(t, _):
+        leave(t, t % LZ, t // LZ).wait()
+        return 0
+
+    lax.fori_loop(0, T, gone, 0)
     best = wl[...]
     for part in range(len(parts)):
         for j in range(1, BUSES):
@@ -484,7 +500,7 @@
             jax.ShapeDtypeStruct((LZ * 4, 128), F32),
         ),
         in_specs=[hbm, hbm, hbm, hbm, hbm, vmem],
-        out_specs=(vmem, vmem),
+        out_specs=(hbm, vmem),
         scratch_shapes=[
             pltpu.SMEM((1, LZ), jnp.int32),
             pltpu.SMEM((SLOTS, LZ), jnp.int32),
@@ -511,6 +527,7 @@
             pltpu.VMEM((T, 2, 4, 16, 256), BF16),
             pltpu.VMEM((T, 4, 16, 128), BF16),
             pltpu.VMEM((T, 4, 16, 256), BF16),
+            pltpu.VMEM((32, LZ * ZL), F32),
             pltpu.VMEM((48, 128), F32),
             pltpu.VMEM((BUSES, 48, 128), F32),
             dma((7,)),
@@ -523,6 +540,7 @@
             dma((T, 4)),
             dma((len(SHARES), BUSES)),
             dma((len(SHARES), BUSES)),
+            dma((T,)),
         ],
         compiler_params=pltpu.CompilerParams(
             collective_id=0, has_side_effects=True, vmem_limit_bytes=62 * 1024 * 1024

time: 88.7 us -> 88.8 us (level)
  no operation moved by 1% of the time
where the time goes in v5:
time: 88.8 us; the launch traced here: 88.6 us
  Pallas kernels  88 us (99%)
    pallas_call x1, Pallas kernels, body(): pl.pallas_call(kernel, out_shape=(jax.ShapeDtypeStruct((32, LZ * ZL), F32...  86 us
    pallas_call x1, Pallas kernels, body(): pl.pallas_call(hand_over, out_shape=(jax.ShapeDtypeStruct((32, LZ * ZL),...  2.02 us

profile of v5, /device:TPU:0, one launch (start us, length us, event | category | flops | bytes accessed | tf_op | source)
XLA Modules:
  0.0 88.6 jit_solution(8644312461521693464)
XLA Ops:
  0.6 86.0 %screen.1 = (f32[32,5632]{1,0:T(8,128)}, f32[44,128]{1,0:T(8,128)}) custom-call(s32[1,11]{1,0:T(1,128)} %bitcast.8, s32[3,11]{1,0:T(4,128)} %bitcast.7, f32[64,4096]{1,0:T(8,128)} %values_hbm.1, s32[512,128]{1,0:T(8,128)} %bitcast.5, bf16[11,3,512,640]{3,2,1,0:T(8,128)(2,1)} %blocks_hbm.1, f32[44,128]{1,0:T(8,128)} %bitcast.6), custom_call_target="tpu_custom_call" | custom-call | tf_op jit(solution)/shard_map/screen/pallas_call | solution.py:496
  86.6 2.0 %hand_over.1 = (f32[32,5632]{1,0:T(8,128)}, f32[44,128]{1,0:T(8,128)}) custom-call(f32[32,5632]{1,0:T(8,128)} %get-tuple-element.6.load_in, f32[44,128]{1,0:T(8,128)} %get-tuple-element.7.worst_in), custom_call_target="tpu_custom_call" | custom-call | tf_op jit(solution)/shard_map/hand_over/pallas_call | solution.py:553

commit v6 on v5

--- a/solution.py
+++ b/solution.py
@@ -21,6 +21,7 @@
 ROWS = (48, 32)
 ROWS_ALL = 80
 DIGITS = 32
+SENT = (40, 32)
 CHUNKS = SITE_DEV // 128
 ZONES = 7
 ZB = 640
@@ -170,7 +171,7 @@
                 if j < BUSES - 1:
                     sv[half][j] = packed[i * rows:(i + 1) * rows]
                     pltpu.make_async_remote_copy(
-                        sv[half].at[j], rv[half].at[bus], xs_sem.at[half, j], xr_sem.at[half, bus],
+                        sv[half].at[j, pl.ds(0, SENT[half])], rv[half].at[bus, pl.ds(0, SENT[half])], xs_sem.at[half, j], xr_sem.at[half, bus],
                         device_id=(line, owners[i]), device_id_type=MESH,
                     ).start()
                 else:
@@ -179,10 +180,11 @@
     def received(half):
         for j in range(1, BUSES):
             src = (bus + j) % BUSES
-            pltpu.make_async_copy(rv[half].at[src], rv[half].at[src], xr_sem.at[half, src]).wait()
+            rows = rv[half].at[src, pl.ds(0, SENT[half])]
+            pltpu.make_async_copy(rows, rows, xr_sem.at[half, src]).wait()
 
     def low_digit(k, _):
-        row = rv0[k, pl.ds(DIGITS, 16), :].astype(F32)[1:2]
+        row = rv0[k, pl.ds(DIGITS, 8), :].astype(F32)[1:2]
         bt[:, lanes(k, 256)] = jnp.where(row == iota((256, 256), 0), 1.0, 0.0).astype(BF16)
         return 0
 
@@ -191,7 +193,7 @@
 
             def high_digit(k, _):
                 vals = rv[half][k, pl.ds(0, 32), :]
-                row = rv0[k, pl.ds(DIGITS, 16), :].astype(F32)[0:1]
+                row = rv0[k, pl.ds(DIGITS, 8), :].astype(F32)[0:1]
                 for i in range(9):
                     lhs[pl.ds(i * 32, 32), lanes(k, 256)] = chosen(row, float(part * 9 + i), vals)
                 return 0
@@ -463,7 +465,8 @@
             route(step, number).wait_send()
     for half in range(2):
         for j in range(BUSES - 1):
-            pltpu.make_async_copy(sv[half].at[j], sv[half].at[j], xs_sem.at[half, j]).wait()
+            rows = sv[half].at[j, pl.ds(0, SENT[half])]
+            pltpu.make_async_copy(rows, rows, xs_sem.at[half, j]).wait()
 
     def gone(t, _):
         leave(t, t % LZ, t // LZ).wait()

time: 88.8 us -> 87.5 us (0.985)
  Pallas kernels: 88 us -> 86.6 us
    pallas_call x1, Pallas kernels: 86 us -> 84.6 us  [body(): pl.pallas_call(kernel, out_shape=(jax.ShapeDtypeStruct((32, LZ * ZL), F32...]
where the time goes in v6:
time: 87.5 us; the launch traced here: 87.3 us
  Pallas kernels  86.6 us (99%)
    pallas_call x1, Pallas kernels, body(): pl.pallas_call(kernel, out_shape=(jax.ShapeDtypeStruct((32, LZ * ZL), F32...  84.6 us
    pallas_call x1, Pallas kernels, body(): pl.pallas_call(hand_over, out_shape=(jax.ShapeDtypeStruct((32, LZ * ZL),...  2.02 us

profile of v6, /device:TPU:0, one launch (start us, length us, event | category | flops | bytes accessed | tf_op | source)
XLA Modules:
  0.0 87.3 jit_solution(9598794134018774405)
XLA Ops:
  0.6 84.6 %screen.1 = (f32[32,5632]{1,0:T(8,128)}, f32[44,128]{1,0:T(8,128)}) custom-call(s32[1,11]{1,0:T(1,128)} %bitcast.8, s32[3,11]{1,0:T(4,128)} %bitcast.7, f32[64,4096]{1,0:T(8,128)} %values_hbm.1, s32[512,128]{1,0:T(8,128)} %bitcast.5, bf16[11,3,512,640]{3,2,1,0:T(8,128)(2,1)} %blocks_hbm.1, f32[44,128]{1,0:T(8,128)} %bitcast.6), custom_call_target="tpu_custom_call" | custom-call | tf_op jit(solution)/shard_map/screen/pallas_call | solution.py:499
  85.3 2.0 %hand_over.1 = (f32[32,5632]{1,0:T(8,128)}, f32[44,128]{1,0:T(8,128)}) custom-call(f32[32,5632]{1,0:T(8,128)} %get-tuple-element.6.load_in, f32[44,128]{1,0:T(8,128)} %get-tuple-element.7.worst_in), custom_call_target="tpu_custom_call" | custom-call | tf_op jit(solution)/shard_map/hand_over/pallas_call | solution.py:556
